TPU v7x, 512 devices: a whole 4x8x8 slice. The times are simulated.
512 devices in a mesh: gx: 16 (over y, core), gy: 32 (over z, x).
Axes of the slice: x: 4, y: 8, z: 8, core: 2. Of those that a mesh axis runs over, the one named last changes fastest.
Arguments:
- tensor: float32 [4096, 4096, 8], P('gx', 'gy'), may hold values from -6 to 6
- sketch_one: float32 [4096, 8, 256], P('gy'), may hold values from -0.03125 to 0.03125
- sketch_two: float32 [256, 8, 256], P('gx'), may hold values from -0.125 to 0.125
Outputs:
- basis_one: float32 [4096, 256], P('gx')
- basis_two: float32 [4096, 256], P('gy')
- core: float32 [256, 256, 8], P('gx', 'gy')
All inputs are finite; a program needn't handle non-finite values.
Results may differ from a plain program's by a relative error of at most 0.00008.
Values sent between devices are 32-bit elements; how exact they have to be, the bound alone decides.
No kernel may reach another device: no remote copies, remote signals or barrier semaphores. Data moves between devices by JAX's collectives and lax.ppermute only.
A program may use at most 64 MiB of HBM per device.

v0:
```python
import jax
import jax.numpy as jnp
from jax import lax
from jax.sharding import PartitionSpec as P


def gram_local(matrix):
    return jnp.dot(matrix.T, matrix, precision=lax.Precision.HIGHEST)


def apply_factor(gram_total, matrix):
    factor = jnp.linalg.cholesky(gram_total)
    return lax.linalg.triangular_solve(
        factor, matrix, left_side=False, lower=True, transpose_a=True
    )


def local(tensor, sketch_one, sketch_two):
    rows_one, rows_two, depth = tensor.shape
    width = sketch_one.shape[2]
    unfolded = tensor.reshape(rows_one, rows_two * depth)
    partial_sketch = jnp.dot(
        unfolded, sketch_one.reshape(rows_two * depth, width), precision=lax.Precision.HIGHEST
    )
    first_sketch = lax.psum(partial_sketch, "gy")
    gram_total = lax.psum(gram_local(first_sketch), "gx")
    basis_one = apply_factor(gram_total, first_sketch)
    rank_rows = width // lax.axis_size("gx")
    partial_core = lax.psum_scatter(
        lax.dot_general(
            basis_one, unfolded, (((0,), (0,)), ((), ())), precision=lax.Precision.HIGHEST
        ),
        "gx",
        scatter_dimension=0,
        tiled=True,
    )
    partial_core = partial_core.reshape(rank_rows, rows_two, depth)
    second_part = jnp.einsum(
        "rjk,rkc->jc", partial_core, sketch_two, precision=lax.Precision.HIGHEST
    )
    second_sketch = lax.psum(second_part, "gx")
    gram_second = lax.psum(gram_local(second_sketch), "gy")
    basis_two = apply_factor(gram_second, second_sketch)
    core_terms = jnp.einsum("rjk,js->rsk", partial_core, basis_two, precision=lax.Precision.HIGHEST)
    core = lax.psum_scatter(core_terms, "gy", scatter_dimension=1, tiled=True)
    return (basis_one, basis_two, core)


def solution(mesh):
    in_specs = (P("gx", "gy", None), P("gy", None, None), P("gx", None, None))
    out_specs = (P("gx", None), P("gy", None), P("gx", "gy", None))
    return jax.shard_map(local, mesh=mesh, in_specs=in_specs, out_specs=out_specs, check_vma=False)
```

profile of v0, /device:TPU:8, one launch (start us, length us, event | category | flops | bytes accessed | tf_op | source)
XLA Modules:
  0.0 984.1 jit_solution(10586373455870248084)
XLA Ops:
  7.2 0.0 all-reduce.6.cloned.1.call-start
  7.2 1.8 copy.34
  9.1 2.5 convolution_bitcast_fusion
  11.6 0.0 all-reduce.6.cloned.1.call-update
  11.6 0.0 all-reduce.8.cloned.1.call-start
  11.7 161.8 %all-reduce.6.cloned.1.call-done = f32[256,256]{1,0:T(8,128)} async-done(((f32[256,256]{1,0:T(8,128)}), f32[256,256]{1,0:T(8,128)}) %all-reduce.6.cloned.1.call-update) | async-done | bytes 262160 | tf_op jit(solution)/shard_map/psum | solution.py:25
  173.5 2.3 fusion.22
  175.8 0.0 all-reduce.8.cloned.1.call-update
  175.9 0.2 reduce-scatter.3.cloned.1.call-start
  176.1 110.6 %all-reduce.8.cloned.1.call-done = f32[256,256]{0,1:T(8,128)} async-done(((f32[256,256]{0,1:T(8,128)}), f32[256,256]{0,1:T(8,128)}) %all-reduce.8.cloned.1.call-update) | async-done | bytes 262160 | tf_op jit(solution)/shard_map/psum | solution.py:26
  286.7 1.1 copy.36
  287.9 11.7 %cholesky.130 = f32[128,128]{1,0:T(8,128)S(1)} custom-call(f32[128,128]{1,0:T(8,128)S(1)} %cholesky.194), custom_call_target="Cholesky" | custom-call | tf_op jit(solution)/shard_map/jit(cholesky)/cholesky | solution.py:12
  299.6 9.8 custom-call.17
  309.5 0.2 constant_dynamic-update-slice_fusion.3
  309.7 0.3 convolution_subtract_fusion.3
  310.0 11.7 %cholesky.147 = f32[128,128]{1,0:T(8,128)S(1)} custom-call(f32[128,128]{1,0:T(8,128)S(1)} %convolution_subtract_fusion.3), custom_call_target="Cholesky" | custom-call | tf_op jit(solution)/shard_map/jit(cholesky)/cholesky | solution.py:12
  321.7 0.7 compare_reduce_fusion.2
  323.7 0.1 triangular_solve.97
  323.8 4.2 while.2
  324.1 0.6 fusion.42
  324.6 1.4 bitcast_dynamic-update-slice_fusion.4
  326.0 0.6 fusion.42
  326.6 1.4 bitcast_dynamic-update-slice_fusion.4
  328.0 19.7 %custom-call.14 = f32[2,128,128]{1,2,0:T(8,128)S(1)} custom-call(f32[2,128,128]{2,1,0:T(8,128)S(1)} %get-tuple-element.11), custom_call_target="InvertDiagBlocksLowerTriangular" | custom-call | tf_op jit(solution)/shard_map/triangular_solve | solution.py:13
  347.7 0.3 fusion.5
  348.0 0.4 convolution_subtract_fusion
  348.4 0.3 fusion.14
  348.7 2.0 fusion
  350.8 0.0 reduce-scatter.3.cloned.1.call-update
  350.8 0.0 all-reduce.10.cloned.1.call-start
  350.8 60.1 %reduce-scatter.3.cloned.1.call-done = f32[16,1024]{1,0:T(8,128)} async-done(((f32[256,1024]{1,0:T(8,128)}), f32[16,1024]{1,0:T(8,128)}) %reduce-scatter.3.cloned.1.call-update) | async-done | bytes 65552 | tf_op jit(solution)/shard_map/reduce_scatter | solution.py:29
  411.0 1.0 copy.38
  412.0 0.2 copy.39
  412.2 0.7 copy-done.5
  412.9 1.0 convolution_bitcast_fusion.2
  413.9 0.0 all-reduce.12.cloned.1.call-start
  414.0 115.5 %all-reduce.10.cloned.1.call-done = f32[128,256]{1,0:T(8,128)} async-done(((f32[128,256]{1,0:T(8,128)}), f32[128,256]{1,0:T(8,128)}) %all-reduce.10.cloned.1.call-update) | async-done | bytes 131088 | tf_op jit(solution)/shard_map/psum | solution.py:41
  529.4 2.1 fusion.23
  531.5 0.0 all-reduce.12.cloned.1.call-update
  531.5 0.0 reduce-scatter.5.cloned.1.call-start
  531.6 161.2 %all-reduce.12.cloned.1.call-done = f32[256,256]{0,1:T(8,128)} async-done(((f32[256,256]{0,1:T(8,128)}), f32[256,256]{0,1:T(8,128)}) %all-reduce.12.cloned.1.call-update) | async-done | bytes 262160 | tf_op jit(solution)/shard_map/psum | solution.py:42
  692.8 1.1 copy.41
  694.0 11.7 %cholesky.164 = f32[128,128]{1,0:T(8,128)S(1)} custom-call(f32[128,128]{1,0:T(8,128)S(1)} %cholesky.197), custom_call_target="Cholesky" | custom-call | tf_op jit(solution)/shard_map/jit(cholesky)/cholesky | solution.py:12
  705.8 9.8 custom-call.18
  715.6 0.2 constant_dynamic-update-slice_fusion.1
  715.8 0.3 convolution_subtract_fusion.2
  716.1 11.7 %cholesky.181 = f32[128,128]{1,0:T(8,128)S(1)} custom-call(f32[128,128]{1,0:T(8,128)S(1)} %convolution_subtract_fusion.2), custom_call_target="Cholesky" | custom-call | tf_op jit(solution)/shard_map/jit(cholesky)/cholesky | solution.py:12
  727.8 0.6 compare_reduce_fusion
  728.5 0.6 compare_reduce_fusion.1
  730.5 4.3 while.3
  730.8 0.6 fusion.43
  731.3 1.4 bitcast_dynamic-update-slice_fusion.5
  732.8 0.6 fusion.43
  733.3 1.4 bitcast_dynamic-update-slice_fusion.5
  734.7 19.7 %custom-call.15 = f32[2,128,128]{1,2,0:T(8,128)S(1)} custom-call(f32[2,128,128]{2,1,0:T(8,128)S(1)} %get-tuple-element.19), custom_call_target="InvertDiagBlocksLowerTriangular" | custom-call | tf_op jit(solution)/shard_map/triangular_solve | solution.py:13
  754.4 0.3 fusion.10
  754.7 0.3 convolution_subtract_fusion.1
  755.0 0.3 fusion.8
  755.3 1.0 convolution_bitcast_fusion.1
  756.3 1.3 copy.44
  757.6 0.0 reduce-scatter.5.cloned.1.call-update
  757.7 0.8 copy.45
  758.5 0.8 copy.46
  759.3 218.0 %reduce-scatter.5.cloned.1.call-done = f32[16,8,8]{0,2,1:T(8,128)} async-done(((f32[16,256,8]{0,2,1:T(8,128)}), f32[16,8,8]{0,2,1:T(8,128)}) %reduce-scatter.5.cloned.1.call-update) | async-done | bytes 4112 | tf_op jit(solution)/shard_map/reduce_scatter | solution.py:45
  (33 shorter events, 0.5 us)
Async XLA Ops:
  7.2 1.9 copy-start
  7.2 166.3 %all-reduce.6.cloned.1.call-start = ((), (), s32[]{:S(2)}) async-start(), calls=%async_computation.2 | async-start | bytes 524288 | tf_op jit(solution)/shard_map/psum | solution.py:25
  11.6 275.0 %all-reduce.8.cloned.1.call-start = ((), (), s32[]{:S(2)}) async-start(), calls=%async_computation.3 | async-start | bytes 524288 | tf_op jit(solution)/shard_map/psum | solution.py:26
  175.9 235.1 %reduce-scatter.3.cloned.1.call-start = ((), (), s32[]{:S(2)}) async-start(), calls=%async_computation.4 | async-start | bytes 1114112 | tf_op jit(solution)/shard_map/reduce_scatter | solution.py:29
  286.7 1.2 copy-start.3
  323.8 23.9 %copy-start.1 = (f32[256,256]{1,0:T(8,128)S(1)}, f32[256,256]{1,0:T(8,128)}, u32[]{:S(2)}) copy-start(f32[256,256]{1,0:T(8,128)} %all-reduce.6.cloned.1.call-done) | copy-start | bytes 786436
  350.8 178.6 %all-reduce.10.cloned.1.call-start = ((), (), s32[]{:S(2)}) async-start(), calls=%async_computation.5 | async-start | bytes 262144 | tf_op jit(solution)/shard_map/psum | solution.py:41
  412.0 0.9 copy-start.5
  413.9 278.9 %all-reduce.12.cloned.1.call-start = ((), (), s32[]{:S(2)}) async-start(), calls=%async_computation.6 | async-start | bytes 524288 | tf_op jit(solution)/shard_map/psum | solution.py:42
  531.5 445.7 %reduce-scatter.5.cloned.1.call-start = ((), (), s32[]{:S(2)}) async-start(), calls=%async_computation.7 | async-start | bytes 1081344 | tf_op jit(solution)/shard_map/reduce_scatter | solution.py:45
  692.8 1.2 copy-start.4
  730.5 24.0 %copy-start.2 = (f32[128,256]{1,0:T(8,128)S(1)}, f32[128,256]{1,0:T(8,128)}, u32[]{:S(2)}) copy-start(f32[128,256]{1,0:T(8,128)} %all-reduce.10.cloned.1.call-done) | copy-start | bytes 393220
Sparse Core Ops, SparseCore 0:
  12.0 161.4 all-reduce.5
  176.4 110.2 all-reduce.7
  350.9 59.9 reduce-scatter.2
  414.0 115.3 all-reduce.9
  533.3 159.4 all-reduce.11
  757.8 219.4 reduce-scatter.4
where the time goes:
time: 985 us; the launch traced here: 984 us
  waiting for transfers between devices  827 us (84%)
  other arithmetic  108 us (11%)
  local copies, waits for them, and re-layouts  17 us (2%)
  between operations  17 us (2%)
  matrix products  13.7 us (1%)
    reduce_scatter x1, waiting for transfers between devices, local(): core = lax.psum_scatter(core_terms, 'gy', scatter_dimension=1, tiled=True)  218 us
    psum x1, waiting for transfers between devices, local(): first_sketch = lax.psum(partial_sketch, 'gy')  162 us
    psum x1, waiting for transfers between devices, local(): gram_second = lax.psum(gram_local(second_sketch), 'gy')  161 us
    psum x1, waiting for transfers between devices, local(): second_sketch = lax.psum(second_part, 'gx')  115 us
    psum x1, waiting for transfers between devices, local(): gram_total = lax.psum(gram_local(first_sketch), 'gx')  111 us
    another operation x13, other arithmetic, apply_factor(): factor = jnp.linalg.cholesky(gram_total)  68.6 us
    reduce_scatter x1, waiting for transfers between devices, local(): lax.psum_scatter(lax.dot_general(basis_one, unfolded, (((0,), (0,)), ((),...  60.1 us
    another operation x7, other arithmetic, apply_factor(): lax.linalg.triangular_solve(factor, matrix, left_side=False, lower=True,...  39.4 us
  transfers between devices with their start and end apart: 6, of which 6 were waited for; matrix products, arithmetic and copies ran while one was open for 0% of the time, Pallas kernels for 0%

commit v1 on v0

v1 whole, which is shorter than its diff:
```python
import jax
import jax.numpy as jnp
from jax import lax
from jax.sharding import PartitionSpec as P

HI = lax.Precision.HIGHEST


def swap(pieces, axis):
    return lax.all_to_all(pieces, axis, 0, 0, tiled=True)


def sum_scatter(total, axis):
    parts = lax.axis_size(axis)
    pieces = total.reshape((parts, total.shape[0] // parts) + total.shape[1:])
    return swap(pieces, axis).sum(0)


def gather(piece, axis):
    parts = lax.axis_size(axis)
    got = swap(jnp.broadcast_to(piece[None], (parts,) + piece.shape), axis)
    return got.reshape((parts * piece.shape[0],) + piece.shape[1:])


def inverse_factor(gram):
    factor = jnp.linalg.cholesky(gram)
    eye = jnp.eye(gram.shape[0], dtype=gram.dtype)
    return lax.linalg.triangular_solve(factor, eye, left_side=False, lower=True, transpose_a=True)


def local(tensor, sketch_one, sketch_two):
    rows_one, rows_two, depth = tensor.shape
    width = sketch_one.shape[2]
    gx, gy = lax.axis_size("gx"), lax.axis_size("gy")
    cells = rows_two // gx
    rank_rows = width // gx
    cols = width // gy

    sketch_all = gather(sketch_two, "gx")

    part = jnp.einsum("ijk,jkc->ic", tensor, sketch_one, precision=HI)
    first = gather(sum_scatter(part, "gy"), "gy")

    gram_part = lax.dot_general(first, first, (((0,), (0,)), ((), ())), precision=HI)
    gram = gather(sum_scatter(gram_part, "gx"), "gx")
    mixed_part = jnp.einsum("ijk,ir->jkr", tensor, first, precision=HI)
    mixed_part, gram = lax.optimization_barrier((mixed_part, gram))
    mixed = sum_scatter(mixed_part, "gx")

    inv_one = inverse_factor(gram)
    basis_one = jnp.dot(first, inv_one, precision=HI)
    core_t = jnp.einsum("jkr,rs->jks", mixed, inv_one, precision=HI)
    second_own = jnp.einsum("jks,skc->jc", core_t, sketch_all, precision=HI)

    share = jnp.transpose(core_t.reshape(cells, depth, gx, rank_rows), (2, 0, 3, 1))
    share = share.reshape(gx, cells * rank_rows * depth // width, width)
    own = jnp.broadcast_to(second_own[None], (gx, cells, width))
    got = swap(jnp.concatenate([own, share], axis=1), "gx")
    second = got[:, :cells].reshape(rows_two, width)
    core_rows = got[:, cells:].reshape(rows_two, rank_rows * depth)

    left = jnp.concatenate([second, core_rows], axis=1)
    both_part = lax.dot_general(left, second, (((0,), (0,)), ((), ())), precision=HI)
    both = gather(sum_scatter(both_part, "gy"), "gy")
    inv_two = inverse_factor(both[:width])
    basis_two = jnp.dot(second, inv_two, precision=HI)
    mine = lax.dynamic_slice_in_dim(inv_two, lax.axis_index("gy") * cols, cols, 1)
    core = jnp.dot(both[width:], mine, precision=HI).reshape(rank_rows, depth, cols)
    return (basis_one, basis_two, jnp.swapaxes(core, 1, 2))


def solution(mesh):
    in_specs = (P("gx", "gy", None), P("gy", None, None), P("gx", None, None))
    out_specs = (P("gx", None), P("gy", None), P("gx", "gy", None))
    return jax.shard_map(local, mesh=mesh, in_specs=in_specs, out_specs=out_specs, check_vma=False)
```

time: 985 us -> 335 us (0.34)
  the two profiles are of different devices: /device:TPU:8 before, /device:TPU:2 now
where the time goes in v1:
time: 335 us; the launch traced here: 330 us
  other arithmetic  116 us (35%)
  blocking collectives  75.4 us (23%)
  waiting for transfers between devices  51.8 us (15%)
  starting transfers between devices  32 us (10%)
  local copies, waits for them, and re-layouts  29.6 us (9%)
  matrix products  21.5 us (6%)
  between operations  3.89 us (1%)
    all_to_all x4, blocking collectives, swap(): return lax.all_to_all(pieces, axis, 0, 0, tiled=True)  75.4 us
    another operation x13, other arithmetic, inverse_factor(): factor = jnp.linalg.cholesky(gram)  69.8 us
    all_to_all x5, waiting for transfers between devices, swap(): return lax.all_to_all(pieces, axis, 0, 0, tiled=True)  51.8 us
    another operation x5, other arithmetic, inverse_factor(): lax.linalg.triangular_solve(factor, eye, left_side=False, lower=True, tra...  41.9 us
    all_to_all x5, starting transfers between devices, swap(): return lax.all_to_all(pieces, axis, 0, 0, tiled=True)  32 us
    another operation x15, local copies, waits for them, and re-layouts, inverse_factor(): lax.linalg.triangular_solve(factor, eye, left_side=False, lower=True, tra...  9.7 us
  transfers between devices with their start and end apart: 5, of which 4 were waited for; matrix products, arithmetic and copies ran while one was open for 25% of the time, Pallas kernels for 0%

profile of v1, /device:TPU:2, one launch (start us, length us, event | category | flops | bytes accessed | tf_op | source)
XLA Modules:
  0.0 330.1 jit_solution(16725416715237643639)
XLA Ops:
  0.6 1.8 copy.34
  2.5 2.5 convolution_bitcast_fusion.1
  5.0 13.5 %all-to-all-start = ((f32[32,8,256]{2,1,0:T(8,128)}), f32[32,8,256]{2,1,0:T(8,128)S(1)}, u32[]{:S(2)}, u32[]{:S(2)}) async-start(f32[32,8,256]{2,1,0:T(8,128)} %convolution_bitcast_fusion.1), calls=%async_computation | async-start | bytes 524288 | tf_op jit(solution)/shard_map/all_to_all | solution.py:10
  18.5 11.2 %all-to-all-done = f32[32,8,256]{2,1,0:T(8,128)S(1)} async-done(((f32[32,8,256]{2,1,0:T(8,128)}), f32[32,8,256]{2,1,0:T(8,128)S(1)}, u32[]{:S(2)}, u32[]{:S(2)}) %all-to-all-start) | async-done | bytes 262176 | tf_op jit(solution)/shard_map/all_to_all | solution.py:10
  29.8 15.8 %all_to_all.45 = f32[32,8,256]{2,1,0:T(8,128)S(1)} all-to-all(f32[32,8,256]{2,1,0:T(8,128)S(1)} %broadcast_in_dim.10), channel_id=1, replica_groups=mesh['gx'=16,'gy'=32] {'gy'}, dimensions={0} | all-to-all | bytes 524288 | tf_op jit(solution)/shard_map/all_to_all | solution.py:10
  46.1 18.2 %all_to_all.47 = f32[16,16,256]{2,1,0:T(8,128)S(1)} all-to-all(f32[16,16,256]{2,1,0:T(8,128)S(1)} %fusion.2), channel_id=1, replica_groups=mesh['gx'=16,'gy'=32] {'gx'}, dimensions={0} | all-to-all | bytes 524288 | tf_op jit(solution)/shard_map/all_to_all | solution.py:10
  64.3 0.7 broadcast_in_dim.11
  65.0 3.5 %all-to-all-start.3 = ((f32[16,16,256]{2,1,0:T(8,128)}), f32[16,16,256]{2,1,0:T(8,128)S(1)}, u32[]{:S(2)}, u32[]{:S(2)}) async-start(f32[16,16,256]{2,1,0:T(8,128)} %broadcast_in_dim.11), calls=%async_computation.3 | async-start | bytes 524288 | tf_op jit(solution)/shard_map/all_to_all | solution.py:10
  68.6 11.3 %all-to-all-done.3 = f32[16,16,256]{2,1,0:T(8,128)S(1)} async-done(((f32[16,16,256]{2,1,0:T(8,128)}), f32[16,16,256]{2,1,0:T(8,128)S(1)}, u32[]{:S(2)}, u32[]{:S(2)}) %all-to-all-start.3) | async-done | bytes 262176 | tf_op jit(solution)/shard_map/all_to_all | solution.py:10
  79.9 1.6 broadcast_in_dim.12
  81.5 4.2 %all-to-all-start.5 = ((f32[16,16,8,256]{3,1,2,0:T(8,128)}), f32[16,16,8,256]{3,1,2,0:T(8,128)S(1)}, u32[]{:S(2)}, u32[]{:S(2)}) async-start(f32[16,16,8,256]{3,1,2,0:T(8,128)} %broadcast_in_dim.12), calls=%async_computation.5 | async-start | bytes 4194304 | tf_op jit(solution)/shard_map/all_to_all | solution.py:10
  85.7 0.7 fusion.11
  86.4 3.4 %convolution_bitcast_fusion = f32[128,8,256]{0,2,1:T(8,128)} fusion(f32[256,128,8]{1,2,0:T(8,128)} %param.6, f32[32,8,256]{2,1,0:T(8,128)S(1)} %all_to_all.45), kind=kOutput, calls=%fused_computation.4 | convolution fusion | flops 805306368 | bytes 2359296 | tf_op jit(solution)/shard_map/ijk,ir->jkr/dot_general | solution.py:46
  89.8 1.8 copy.38
  91.6 1.1 fusion.8
  92.7 0.7 copy-done.5
  93.4 11.7 %cholesky.130 = f32[128,128]{1,0:T(8,128)S(1)} custom-call(f32[128,128]{1,0:T(8,128)S(1)} %cholesky.194), custom_call_target="Cholesky" | custom-call | tf_op jit(solution)/shard_map/jit(cholesky)/cholesky | solution.py:26
  105.1 0.7 cholesky.155
  105.9 10.4 %custom-call.13 = f32[1,128,128]{1,2,0:T(8,128)} custom-call(f32[1,128,128]{2,1,0:T(8,128)S(1)} %get-tuple-element.58), custom_call_target="InvertDiagBlocksLowerTriangular" | custom-call | tf_op jit(solution)/shard_map/jit(cholesky)/cholesky | solution.py:26
  116.3 2.6 copy.39
  119.0 1.7 constant_dynamic-update-slice_fusion.3
  120.6 14.3 %all-to-all-done.5 = f32[16,16,8,256]{3,1,2,0:T(8,128)S(1)} async-done(((f32[16,16,8,256]{3,1,2,0:T(8,128)}), f32[16,16,8,256]{3,1,2,0:T(8,128)S(1)}, u32[]{:S(2)}, u32[]{:S(2)}) %all-to-all-start.5) | async-done | bytes 2097184 | tf_op jit(solution)/shard_map/all_to_all | solution.py:10
  134.9 4.8 %all-to-all-start.4 = ((f32[16,8,8,256]{3,2,1,0:T(8,128)}), f32[16,8,8,256]{3,2,1,0:T(8,128)}, u32[]{:S(2)}, u32[]{:S(2)}) async-start(f32[16,8,8,256]{3,2,1,0:T(8,128)} %bitcast.113), calls=%async_computation.4 | async-start | bytes 2097152 | tf_op jit(solution)/shard_map/all_to_all | solution.py:10
  139.8 1.1 convolution_subtract_fusion.3
  140.9 11.7 %cholesky.147 = f32[128,128]{1,0:T(8,128)S(1)} custom-call(f32[128,128]{1,0:T(8,128)S(1)} %convolution_subtract_fusion.3), custom_call_target="Cholesky" | custom-call | tf_op jit(solution)/shard_map/jit(cholesky)/cholesky | solution.py:26
  152.6 0.6 select_reduce_fusion.2
  153.2 0.6 compare_reduce_fusion.2
  155.1 1.7 select_select_fusion.1
  156.9 5.6 %while.4 = (s32[]{:T(128)}, f32[256,256]{1,0:T(8,128)}, s32[2,2]{1,0:T(2,128)S(1)}, f32[2,128,128]{2,1,0:T(8,128)S(1)}, s32[]{:T(128)}) while((s32[]{:T(128)}, f32[256,256]{1,0:T(8,128)}, s32[2,2]{1,0:T(2,128)S(1)}, f32[2,128,128]{2,1,0:T(8,128)S(1)}, s32[]{:T(128)}) %tuple.51), condition=%wide.while_cond, body=%wide.while_body.sunk | while | flops 2 | bytes 131189 | solution.py:28
  156.9 0.6 fusion.57
  157.5 2.2 bitcast_dynamic-update-slice_fusion.4
  159.8 0.6 fusion.57
  160.3 2.2 bitcast_dynamic-update-slice_fusion.4
  162.5 20.3 %custom-call.14 = f32[2,128,128]{1,2,0:T(8,128)} custom-call(f32[2,128,128]{2,1,0:T(8,128)S(1)} %get-tuple-element.23), custom_call_target="InvertDiagBlocksLowerTriangular" | custom-call | tf_op jit(solution)/shard_map/triangular_solve/custom-call.0 | solution.py:28
  182.8 1.2 fusion.20
  184.1 1.3 convolution_subtract_fusion.1
  185.4 1.8 fusion.26
  187.2 1.6 copy.42
  188.8 2.1 reduce_sum.38
  190.9 1.9 fusion.6
  192.8 1.8 reshape.70
  194.6 2.1 copy.44
  196.7 1.8 copy.45
  198.5 1.8 convolution_bitcast_fusion.2
  200.4 18.3 %all_to_all.46 = f32[16,12,256]{2,1,0:T(8,128)S(1)} all-to-all(f32[16,12,256]{2,1,0:T(8,128)S(1)} %pad_maximum_fusion.3), channel_id=1, replica_groups=mesh['gx'=16,'gy'=32] {'gx'}, dimensions={0} | all-to-all | bytes 393216 | tf_op jit(solution)/shard_map/all_to_all | solution.py:10
  218.9 0.5 fusion.12
  219.6 23.2 %all_to_all.48 = f32[32,12,256]{2,1,0:T(8,128)S(1)} all-to-all(f32[32,12,256]{2,1,0:T(8,128)S(1)} %copy.48), channel_id=1, replica_groups=mesh['gx'=16,'gy'=32] {'gy'}, dimensions={0} | all-to-all | bytes 786432 | tf_op jit(solution)/shard_map/all_to_all | solution.py:10
  242.9 0.9 broadcast_in_dim.15
  243.7 5.9 %all-to-all-start.8 = ((f32[32,12,256]{2,1,0:T(8,128)}), f32[32,12,256]{2,1,0:T(8,128)S(1)}, u32[]{:S(2)}, u32[]{:S(2)}) async-start(f32[32,12,256]{2,1,0:T(8,128)} %broadcast_in_dim.15), calls=%async_computation.8 | async-start | bytes 1048576 | tf_op jit(solution)/shard_map/all_to_all | solution.py:10
  249.7 1.1 fusion.9
  250.8 15.0 %all-to-all-done.8 = f32[32,12,256]{2,1,0:T(8,128)S(1)} async-done(((f32[32,12,256]{2,1,0:T(8,128)}), f32[32,12,256]{2,1,0:T(8,128)S(1)}, u32[]{:S(2)}, u32[]{:S(2)}) %all-to-all-start.8) | async-done | bytes 393248 | tf_op jit(solution)/shard_map/all_to_all | solution.py:10
  266.1 11.7 %cholesky.164 = f32[128,128]{1,0:T(8,128)S(1)} custom-call(f32[128,128]{1,0:T(8,128)S(1)} %cholesky.197), custom_call_target="Cholesky" | custom-call | tf_op jit(solution)/shard_map/jit(cholesky)/cholesky | solution.py:26
  277.9 9.8 %custom-call.15 = f32[1,128,128]{1,2,0:T(8,128)S(1)} custom-call(f32[1,128,128]{2,1,0:T(8,128)S(1)} %get-tuple-element.54), custom_call_target="InvertDiagBlocksLowerTriangular" | custom-call | tf_op jit(solution)/shard_map/jit(cholesky)/cholesky | solution.py:26
  288.2 11.7 %cholesky.181 = f32[128,128]{1,0:T(8,128)S(1)} custom-call(f32[128,128]{1,0:T(8,128)S(1)} %convolution_subtract_fusion.2), custom_call_target="Cholesky" | custom-call | tf_op jit(solution)/shard_map/jit(cholesky)/cholesky | solution.py:26
  299.9 0.6 compare_reduce_fusion.1
  300.6 0.7 compare_reduce_fusion
  302.7 4.1 %while.5 = (s32[]{:T(128)}, f32[256,256]{1,0:T(8,128)S(1)}, s32[2,2]{1,0:T(2,128)S(1)}, f32[2,128,128]{2,1,0:T(8,128)S(1)}, s32[]{:T(128)}) while((s32[]{:T(128)}, f32[256,256]{1,0:T(8,128)S(1)}, s32[2,2]{1,0:T(2,128)S(1)}, f32[2,128,128]{2,1,0:T(8,128)S(1)}, s32[]{:T(128)}) %tuple.57), condition=%wide.while_cond.clone, body=%wide.while_body.clone.sunk | while | flops 2 | bytes 131189 | solution.py:28
  302.7 0.6 fusion.58
  303.3 1.4 bitcast_dynamic-update-slice_fusion.5
  304.7 0.6 fusion.58
  305.3 1.4 bitcast_dynamic-update-slice_fusion.5
  306.8 19.9 %custom-call.16 = f32[2,128,128]{1,2,0:T(8,128)S(1)} custom-call(f32[2,128,128]{2,1,0:T(8,128)S(1)} %get-tuple-element.24), custom_call_target="InvertDiagBlocksLowerTriangular" | custom-call | tf_op jit(solution)/shard_map/triangular_solve/custom-call.0 | solution.py:28
  328.1 0.7 copy.51
  328.8 1.1 fusion.1
  (60 shorter events, 3.5 us)
Async XLA Ops:
  0.6 1.8 copy-start
  5.0 24.7 %all-to-all-start = ((f32[32,8,256]{2,1,0:T(8,128)}), f32[32,8,256]{2,1,0:T(8,128)S(1)}, u32[]{:S(2)}, u32[]{:S(2)}) async-start(f32[32,8,256]{2,1,0:T(8,128)} %convolution_bitcast_fusion.1), calls=%async_computation | async-start | bytes 524288 | tf_op jit(solution)/shard_map/all_to_all | solution.py:10
  18.5 50.1 %copy-start.7 = (f32[16,8,256]{2,1,0:T(8,128)S(1)}, f32[16,8,256]{2,1,0:T(8,128)}, u32[]{:S(2)}) copy-start(f32[16,8,256]{2,1,0:T(8,128)} %param.8) | copy-start | bytes 393220
  65.0 14.9 %all-to-all-start.3 = ((f32[16,16,256]{2,1,0:T(8,128)}), f32[16,16,256]{2,1,0:T(8,128)S(1)}, u32[]{:S(2)}, u32[]{:S(2)}) async-start(f32[16,16,256]{2,1,0:T(8,128)} %broadcast_in_dim.11), calls=%async_computation.3 | async-start | bytes 524288 | tf_op jit(solution)/shard_map/all_to_all | solution.py:10
  79.9 1.6 copy-start.3
  81.5 53.4 %all-to-all-start.5 = ((f32[16,16,8,256]{3,1,2,0:T(8,128)}), f32[16,16,8,256]{3,1,2,0:T(8,128)S(1)}, u32[]{:S(2)}, u32[]{:S(2)}) async-start(f32[16,16,8,256]{3,1,2,0:T(8,128)} %broadcast_in_dim.12), calls=%async_computation.5 | async-start | bytes 4194304 | tf_op jit(solution)/shard_map/all_to_all | solution.py:10
  92.7 0.7 copy-start.5
  116.3 2.6 copy-start.8
  134.9 53.9 %all-to-all-start.4 = ((f32[16,8,8,256]{3,2,1,0:T(8,128)}), f32[16,8,8,256]{3,2,1,0:T(8,128)}, u32[]{:S(2)}, u32[]{:S(2)}) async-start(f32[16,8,8,256]{3,2,1,0:T(8,128)} %bitcast.113), calls=%async_computation.4 | async-start | bytes 2097152 | tf_op jit(solution)/shard_map/all_to_all | solution.py:10
  188.8 9.7 %copy-start.1 = (f32[16,16,8,256]{3,1,0,2:T(8,128)S(1)}, f32[16,16,8,256]{3,1,0,2:T(8,128)}, u32[]{:S(2)}) copy-start(f32[16,16,8,256]{3,1,0,2:T(8,128)} %copy.42) | copy-start | bytes 6291460
  198.5 1.8 copy-start.6
  219.4 30.3 %copy-start.4 = (f32[256,128]{0,1:T(8,128)S(1)}, f32[256,128]{0,1:T(8,128)}, u32[]{:S(2)}) copy-start(f32[256,128]{0,1:T(8,128)} %fusion.26) | copy-start | bytes 393220
  243.7 22.1 %all-to-all-start.8 = ((f32[32,12,256]{2,1,0:T(8,128)}), f32[32,12,256]{2,1,0:T(8,128)S(1)}, u32[]{:S(2)}, u32[]{:S(2)}) async-start(f32[32,12,256]{2,1,0:T(8,128)} %broadcast_in_dim.15), calls=%async_computation.8 | async-start | bytes 1048576 | tf_op jit(solution)/shard_map/all_to_all | solution.py:10
  265.9 60.8 %copy-start.2 = (f32[256,256]{1,0:T(8,128)S(1)}, f32[256,256]{1,0:T(8,128)}, u32[]{:S(2)}) copy-start(f32[256,256]{1,0:T(8,128)} %fusion.11) | copy-start | bytes 786436

commit v2 on v0

v2 whole, which is shorter than its diff:
```python
import jax
import jax.numpy as jnp
from jax import lax
from jax.experimental import pallas as pl
from jax.experimental.pallas import tpu as pltpu
from jax.sharding import PartitionSpec as P

HI = lax.Precision.HIGHEST
H = 128


def spread_col(x,p):
    return jnp.broadcast_to(x[:,p:p+1],(8,H))


def spread_row(x,r):
    return jnp.broadcast_to(x[r:r+1,:],(8,H))


def eliminate(d_ref,e_ref,x_ref):
    sub=lax.broadcasted_iota(jnp.int32,(8,H),0)
    lane=lax.broadcasted_iota(jnp.int32,(8,H),1)
    for k in range(16):
        rows=slice(8*k,8*k+8)
        block=(lane>=8*k)&(lane<8*k+8)
        Dk=d_ref[rows,:]; Ek=e_ref[rows,:]
        cb=[spread_col(Dk,8*k+t) for t in range(8)]
        s=[[spread_row(cb[t],q) for t in range(q+1)] for q in range(8)]
        Dm=jnp.where(block,jnp.where(lane==8*k+sub,1.0,0.0),Dk)
        rD=[spread_row(Dm,t) for t in range(8)]
        rE=[spread_row(Ek,t) for t in range(8)]
        inv=[None]*8; f=[[None]*8 for _ in range(8)]; W=[[None]*8 for _ in range(8)]
        dsel=s[0][0]
        for j in range(8):
            inv[j]=1.0/s[j][j]
            if j: dsel=jnp.where(sub==j,s[j][j],dsel)
            for q in range(j+1,8):
                f[q][j]=s[q][j]*inv[j]
            for q in range(j+1,8):
                for t in range(j+1,q+1):
                    s[q][t]=s[q][t]-f[q][j]*s[t][j]
        for q in range(8):
            for t in range(q):
                a=f[q][t]
                for m in range(t+1,q):
                    a=a+f[q][m]*W[m][t]
                W[q][t]=-a
        uD=list(rD); uE=list(rE)
        for q in range(1,8):
            for t in range(q):
                uD[q]=uD[q]+W[q][t]*rD[t]
                uE[q]=uE[q]+W[q][t]*rE[t]
        for g in range(k+1,16):
            gr=slice(8*g,8*g+8)
            Dg=d_ref[gr,:]; Eg=e_ref[gr,:]
            c=[spread_col(Dg,8*k+t) for t in range(8)]
            Dg=jnp.where(block,0.0,Dg)
            for j in range(8):
                a=c[j]
                for t in range(j):
                    a=a+W[j][t]*c[t]
                a=a*inv[j]
                Dg=Dg-a*uD[j]; Eg=Eg-a*uE[j]
            d_ref[gr,:]=Dg; e_ref[gr,:]=Eg
        rs=1.0/jnp.sqrt(dsel)
        nD=uD[0]; nE=uE[0]
        for q in range(1,8):
            nD=jnp.where(sub==q,uD[q],nD); nE=jnp.where(sub==q,uE[q],nE)
        row=8*k+sub
        x_ref[rows,:]=jnp.where(lane<=row,nD,0.0)*rs
        e_ref[rows,:]=nE*rs


def dot0(a,b):
    return lax.dot_general(a,b,(((0,),(0,)),((),())),precision=HI,preferred_element_type=jnp.float32)


def dot_t(a, b):
    return lax.dot_general(a, b, (((1,), (1,)), ((), ())), precision=HI, preferred_element_type=jnp.float32)


def factor_rows(g_ref, o_ref, d_ref, e_ref, x_ref):
    d_ref[...] = g_ref[:H, :H]
    e_ref[...] = g_ref[:H, H:]

    def body(b, carry):
        eliminate(d_ref, e_ref, x_ref)

        @pl.when(b == 0)
        def _():
            o_ref[:H, :H] = x_ref[...]
            o_ref[:H, H:] = jnp.zeros((H, H), jnp.float32)
            u = e_ref[...]
            d_ref[...] = g_ref[H:, H:] - dot0(u, u)
            e_ref[...] = -dot0(u, x_ref[...])

        return carry

    lax.fori_loop(0, 2, body, 0)
    o_ref[H:, H:] = x_ref[...]
    o_ref[H:, :H] = e_ref[...]


def first_factor_kernel(i_ref, g_ref, o_ref, p_ref, d_ref, e_ref, x_ref):
    factor_rows(g_ref, o_ref, d_ref, e_ref, x_ref)
    me = i_ref[0]
    y, c = me >> 1, me & 1
    for b in range(16):
        their_y, their_c = b // 2, b % 2
        step = (y - their_y) if their_c == 0 else (their_y - y)
        place = 8 * (c ^ their_c) + (step & 7)
        p_ref[pl.ds(pl.multiple_of(16 * place, 16), 16), :] = o_ref[16 * b : 16 * b + 16, :]


def second_factor_kernel(g_ref, left_ref, o_ref, b_ref, d_ref, e_ref, x_ref):
    factor_rows(g_ref, o_ref, d_ref, e_ref, x_ref)
    b_ref[...] = dot_t(left_ref[:, :256], o_ref[...])


def second_sketch_kernel(m_ref, x_ref, p_ref, s_ref, t_ref, o_ref):
    mixed = m_ref[0]
    for i in range(1, 8):
        mixed = mixed + m_ref[i]
    placed = dot_t(mixed, p_ref[...])
    second = jnp.zeros((8, 256), jnp.float32)
    for k in range(8):
        rows = placed[8 * k : 8 * k + 8]
        for half, ref in enumerate((s_ref, t_ref)):
            block = ref[:, k].reshape(H, 256)
            second = second + jnp.dot(
                rows[:, H * half : H * half + H], block, precision=HI, preferred_element_type=jnp.float32
            )
    core = dot_t(mixed, x_ref[...])
    lane = lax.broadcasted_iota(jnp.int32, (8, H), 1)
    for m in range(16):
        chunk = jnp.zeros((8, H), jnp.float32)
        for k in range(8):
            half = core[8 * k : 8 * k + 8, H * (m // 8) : H * (m // 8) + H]
            shift = (16 * (k - m % 8)) % H
            moved = pltpu.roll(half, shift, 1) if shift else half
            chunk = jnp.where((lane >= 16 * k) & (lane < 16 * k + 16), moved, chunk)
        o_ref[m, :, :256] = second
        o_ref[m, :, 256:] = chunk


VMEM = pl.BlockSpec(memory_space=pltpu.VMEM)
SMEM = pl.BlockSpec(memory_space=pltpu.SMEM)
SQUARE = jax.ShapeDtypeStruct((256, 256), jnp.float32)
SCRATCH = [pltpu.VMEM((H, H), jnp.float32)] * 3
FACTOR_COST = pl.CostEstimate(flops=6_000_000_000, bytes_accessed=786432, transcendentals=0)


def first_factor(index, gram):
    return pl.pallas_call(
        first_factor_kernel,
        out_shape=(SQUARE, SQUARE),
        in_specs=[SMEM, VMEM],
        out_specs=(VMEM, VMEM),
        scratch_shapes=SCRATCH,
        cost_estimate=FACTOR_COST,
        name="first_factor",
    )(index, gram)


def second_factor(gram, left):
    return pl.pallas_call(
        second_factor_kernel,
        out_shape=(SQUARE, jax.ShapeDtypeStruct((128, 256), jnp.float32)),
        in_specs=[VMEM, VMEM],
        out_specs=(VMEM, VMEM),
        scratch_shapes=SCRATCH,
        cost_estimate=FACTOR_COST,
        name="second_factor",
    )(gram, left)


def second_sketch(mixed, inverse, placed, near, far):
    return pl.pallas_call(
        second_sketch_kernel,
        out_shape=jax.ShapeDtypeStruct((16, 8, 384), jnp.float32),
        in_specs=[VMEM] * 5,
        out_specs=VMEM,
        cost_estimate=pl.CostEstimate(flops=200_000_000, bytes_accessed=4_000_000, transcendentals=0),
        name="second_sketch",
    )(mixed, inverse, placed, near, far)


def swap(pieces, axis, groups=None):
    return lax.all_to_all(pieces, axis, 0, 0, axis_index_groups=groups, tiled=True)


def sum_scatter(pieces, axis):
    return swap(pieces, axis).sum(0)


def spread(piece, axis):
    return swap(jnp.broadcast_to(piece[None], (lax.axis_size(axis),) + piece.shape), axis)


def local(tensor, sketch_one, sketch_two):
    gx, gy = 16, 32
    row, col = lax.axis_index("gx"), lax.axis_index("gy")
    core_of = row % 2
    twin = [(i, i ^ 1) for i in range(gx)]

    def turn(d):
        return [(2 * y + c, 2 * ((y + (d if c == 0 else -d)) % 8) + c) for y in range(8) for c in range(2)]

    near = jnp.swapaxes(sketch_two, 0, 1)[None]
    for d in (1, 2, 4):
        near = jnp.concatenate([near, lax.ppermute(near, "gx", turn(d))], axis=0)
    far = lax.ppermute(near, "gx", twin)

    part = jnp.einsum("ijk,jkc->ic", tensor, sketch_one, precision=HI)
    first_own = sum_scatter(part.reshape(gy, 8, 256), "gy")
    first = spread(first_own, "gy").reshape(256, 256)

    gram_part = lax.dot_general(first, first, (((0,), (0,)), ((), ())), precision=HI)
    gram_own = spread(lax.dynamic_slice_in_dim(gram_part, 8 * col, 8, 0), "gx").sum(0)
    gram = spread(gram_own, "gy").reshape(256, 256)

    mixed_part = jnp.einsum("ijk,ir->kjr", tensor, first, precision=HI)
    mixed_part = mixed_part.reshape(8, 8, 2, 8, 256).transpose(2, 1, 0, 3, 4).reshape(2, 8, 64, 256)
    keep = lax.dynamic_index_in_dim(mixed_part, core_of, 0, keepdims=False)
    give = lax.dynamic_index_in_dim(mixed_part, 1 - core_of, 0, keepdims=False)
    mixed_half = keep + lax.ppermute(give, "gx", twin)
    mixed_half, gram = lax.optimization_barrier((mixed_half, gram))
    mixed = swap(mixed_half, "gx", [list(range(0, gx, 2)), list(range(1, gx, 2))])

    inv_one, placed = first_factor(row.astype(jnp.int32)[None], gram)
    basis_one = jnp.einsum("it,st->is", first, inv_one, precision=HI)
    out = second_sketch(mixed, inv_one, placed, near, far)
    left = swap(out, "gx").reshape(128, 384)

    both_part = lax.dot_general(left[:, :256], left, (((0,), (0,)), ((), ())), precision=HI)
    both_own = sum_scatter(both_part.reshape(gy, 8, 384), "gy")
    gram_two = spread(both_own[:, :256], "gy").reshape(256, 256)
    core_own, gram_two = lax.optimization_barrier((both_own[:, 256:], gram_two))
    core_in = spread(core_own, "gy").reshape(256, 128)
    inv_two, basis_two = second_factor(gram_two, left)
    mine = lax.dynamic_slice_in_dim(inv_two, 8 * col, 8, 0)
    core = jnp.dot(mine, core_in, precision=HI).reshape(8, 8, 16)
    return (basis_one, basis_two, jnp.transpose(core, (2, 0, 1)))


def solution(mesh):
    in_specs = (P("gx", "gy", None), P("gy", None, None), P("gx", None, None))
    out_specs = (P("gx", None), P("gy", None), P("gx", "gy", None))
    return jax.shard_map(local, mesh=mesh, in_specs=in_specs, out_specs=out_specs, check_vma=False)
```

time: 985 us -> 204 us (0.21)
  the two profiles are of different devices: /device:TPU:8 before, /device:TPU:2 now
where the time goes in v2:
time: 204 us; the launch traced here: 203 us
  starting transfers between devices  67.9 us (33%)
  blocking collectives  52 us (25%)
  waiting for transfers between devices  35.6 us (17%)
  Pallas kernels  26.8 us (13%)
  local copies, waits for them, and re-layouts  8.58 us (4%)
  matrix products  7.79 us (4%)
  other arithmetic  3.29 us (2%)
    all_to_all x3, blocking collectives, swap(): lax.all_to_all(pieces, axis, 0, 0, axis_index_groups=groups, tiled=True)  52 us
    all_to_all x6, starting transfers between devices, swap(): lax.all_to_all(pieces, axis, 0, 0, axis_index_groups=groups, tiled=True)  45.6 us
    all_to_all x6, waiting for transfers between devices, swap(): lax.all_to_all(pieces, axis, 0, 0, axis_index_groups=groups, tiled=True)  28.6 us
    ppermute x3, starting transfers between devices, local(): near = jnp.concatenate([near, lax.ppermute(near, 'gx', turn(d))], axis=0)  17.4 us
    pallas_call x1, Pallas kernels, second_factor(): pl.pallas_call(second_factor_kernel, out_shape=(SQUARE, jax.ShapeDtypeStr...  11.4 us
    pallas_call x1, Pallas kernels, first_factor(): pl.pallas_call(first_factor_kernel, out_shape=(SQUARE, SQUARE), in_specs=...  11 us
    ppermute x3, waiting for transfers between devices, local(): near = jnp.concatenate([near, lax.ppermute(near, 'gx', turn(d))], axis=0)  6.92 us
    unnamed x23, local copies, waits for them, and re-layouts  4.56 us
  transfers between devices with their start and end apart: 11, of which 5 were waited for; matrix products, arithmetic and copies ran while one was open for 5% of the time, Pallas kernels for 11%

profile of v2, /device:TPU:2, one launch (start us, length us, event | category | flops | bytes accessed | tf_op | source)
XLA Modules:
  0.0 202.9 jit_solution(1548962855353583639)
XLA Ops:
  0.6 0.0 copy-start
  0.6 1.8 copy.33
  2.5 0.0 copy-done
  2.5 2.5 %convolution_bitcast_fusion.1 = f32[32,8,256]{2,1,0:T(8,128)} fusion(f32[256,128,8]{0,2,1:T(8,128)S(1)} %copy.33, f32[128,8,256]{2,1,0:T(8,128)S(1)} %copy-done), kind=kOutput, calls=%fused_computation.1 | convolution fusion | flops 805306368 | bytes 2359296 | tf_op jit(solution)/shard_map/ijk,jkc->ic/dot_general | solution.py:214
  5.0 0.0 copy-start.9
  5.0 13.6 %all-to-all-start = ((f32[32,8,256]{2,1,0:T(8,128)}), f32[32,8,256]{2,1,0:T(8,128)S(1)}, u32[]{:S(2)}, u32[]{:S(2)}) async-start(f32[32,8,256]{2,1,0:T(8,128)} %convolution_bitcast_fusion.1), calls=%async_computation | async-start | bytes 524288 | tf_op jit(solution)/shard_map/all_to_all | solution.py:189
  18.6 0.0 copy-done.9
  18.7 3.5 %collective-permute-start.1 = (f32[1,8,16,256]{3,2,1,0:T(8,128)S(1)}, f32[1,8,16,256]{3,2,1,0:T(8,128)S(1)}, u32[]{:S(2)}, u32[]{:S(2)}) collective-permute-start(f32[1,8,16,256]{3,2,1,0:T(8,128)S(1)} %bitcast.61), channel_id=1, source_target_pairs={{0,64},{32,480},{64,128},{96,32},{128,192},{160,96},{192,256},{224... | collective-permute-start | bytes 393224 | tf_op jit(solution)/shard_map/ppermute | solution.py:211
  22.2 7.7 %all-to-all-done = f32[32,8,256]{2,1,0:T(8,128)S(1)} async-done(((f32[32,8,256]{2,1,0:T(8,128)}), f32[32,8,256]{2,1,0:T(8,128)S(1)}, u32[]{:S(2)}, u32[]{:S(2)}) %all-to-all-start) | async-done | bytes 262176 | tf_op jit(solution)/shard_map/all_to_all | solution.py:189
  29.9 0.7 broadcast_in_dim.14
  30.6 0.0 copy-start.2
  30.6 5.7 %all-to-all-start.1 = ((f32[32,8,256]{2,1,0:T(8,128)}), f32[32,8,256]{2,1,0:T(8,128)S(1)}, u32[]{:S(2)}, u32[]{:S(2)}) async-start(f32[32,8,256]{2,1,0:T(8,128)} %broadcast_in_dim.14), calls=%async_computation.1 | async-start | bytes 524288 | tf_op jit(solution)/shard_map/all_to_all | solution.py:189
  36.3 0.0 collective-permute-done.1
  36.3 0.0 copy-start.5
  36.4 4.5 %collective-permute-start.2 = (f32[2,8,16,256]{3,2,1,0:T(8,128)S(1)}, f32[2,8,16,256]{3,2,1,0:T(8,128)S(1)}, u32[]{:S(2)}, u32[]{:S(2)}) collective-permute-start(f32[2,8,16,256]{3,2,1,0:T(8,128)S(1)} %pad_maximum_fusion.2), channel_id=1, source_target_pairs={{0,128},{32,416},{64,192},{96,480},{128,256},{160,32},{192,320},{2... | collective-permute-start | bytes 786440 | tf_op jit(solution)/shard_map/ppermute | solution.py:211
  40.9 6.9 %collective-permute-done.2 = f32[2,8,16,256]{3,2,1,0:T(8,128)S(1)} collective-permute-done((f32[2,8,16,256]{3,2,1,0:T(8,128)S(1)}, f32[2,8,16,256]{3,2,1,0:T(8,128)S(1)}, u32[]{:S(2)}, u32[]{:S(2)}) %collective-permute-start.2) | collective-permute-done | bytes 262176 | tf_op jit(solution)/shard_map/ppermute | solution.py:211
  47.8 0.0 copy-done.5
  47.8 0.0 copy-start.7
  47.8 0.7 copy-done.7
  48.5 9.4 %collective-permute-start.3 = (f32[4,8,16,256]{3,2,1,0:T(8,128)S(1)}, f32[4,8,16,256]{3,2,1,0:T(8,128)}, u32[]{:S(2)}, u32[]{:S(2)}) collective-permute-start(f32[4,8,16,256]{3,2,1,0:T(8,128)S(1)} %pad_maximum_fusion.1), channel_id=1, source_target_pairs={{0,256},{32,288},{64,320},{96,352},{128,384},{160,416},{192,448},{... | collective-permute-start | bytes 1572872 | tf_op jit(solution)/shard_map/ppermute | solution.py:211
  57.9 0.0 all-to-all-done.1
  57.9 0.0 copy-done.2
  57.9 1.8 fusion
  59.8 0.1 copy.44
  59.9 0.8 dynamic-slice_bitcast_fusion
  60.7 1.9 collective-permute-start
  62.6 0.6 convolution_bitcast_fusion
  63.3 17.9 %all_to_all.45 = f32[16,8,256]{2,1,0:T(8,128)S(1)} all-to-all(f32[16,8,256]{2,1,0:T(8,128)S(1)} %broadcast_in_dim.16), channel_id=1, replica_groups=mesh['gx'=16,'gy'=32] {'gx'}, dimensions={0} | all-to-all | bytes 262144 | tf_op jit(solution)/shard_map/all_to_all | solution.py:189
  81.2 0.7 broadcast_in_dim.17
  81.9 9.8 %all-to-all-start.3 = ((f32[32,8,256]{2,1,0:T(8,128)}), f32[32,8,256]{2,1,0:T(8,128)}, u32[]{:S(2)}, u32[]{:S(2)}) async-start(f32[32,8,256]{2,1,0:T(8,128)} %broadcast_in_dim.17), calls=%async_computation.3 | async-start | bytes 524288 | tf_op jit(solution)/shard_map/all_to_all | solution.py:189
  91.8 0.0 collective-permute-done.3
  91.8 1.2 pad_maximum_fusion.s_ref
  93.1 0.0 copy-start.1
  93.1 3.0 %collective-permute-start.4 = (f32[8,8,16,256]{3,2,1,0:T(8,128)S(1)}, f32[8,8,16,256]{3,2,1,0:T(8,128)}, u32[]{:S(2)}, u32[]{:S(2)}) collective-permute-start(f32[8,8,16,256]{3,2,1,0:T(8,128)S(1)} %pad_maximum_fusion.s_ref), channel_id=1, source_target_pairs={{0,32},{32,0},{64,96},{96,64},{128,160},{160,128},{192,224},{224,1... | collective-permute-start | bytes 3145736 | tf_op jit(solution)/shard_map/ppermute | solution.py:212
  96.1 0.0 collective-permute-done
  96.1 1.9 bitcast_add_fusion
  98.0 5.9 %all-to-all-done.3 = f32[32,8,256]{2,1,0:T(8,128)} async-done(((f32[32,8,256]{2,1,0:T(8,128)}), f32[32,8,256]{2,1,0:T(8,128)}, u32[]{:S(2)}, u32[]{:S(2)}) %all-to-all-start.3) | async-done | bytes 262176 | tf_op jit(solution)/shard_map/all_to_all | solution.py:189
  103.9 0.0 copy-done.1
  103.9 5.2 %all-to-all-start.4 = ((f32[8,64,256]{2,1,0:T(8,128)}), f32[8,64,256]{2,1,0:T(8,128)S(1)}, u32[]{:S(2)}, u32[]{:S(2)}) async-start(f32[8,64,256]{2,1,0:T(8,128)} %bitcast_add_fusion), calls=%async_computation.4 | async-start | bytes 1048576 | tf_op jit(solution)/shard_map/all_to_all | solution.py:189
  109.2 11.0 %first_factor.1 = (f32[256,256]{1,0:T(8,128)}, f32[256,256]{1,0:T(8,128)}) custom-call(s32[1]{0:T(128)} %bitcast.3.i_ref, f32[256,256]{1,0:T(8,128)} %bitcast.12.g_ref), custom_call_target="tpu_custom_call" | custom-call | flops 6000000000 | bytes 786432 | tf_op jit(solution)/shard_map/first_factor/pallas_call | solution.py:154
  120.2 0.0 collective-permute-done.4.t_ref
  120.2 5.4 %all-to-all-done.4.m_ref = f32[8,64,256]{2,1,0:T(8,128)S(1)} async-done(((f32[8,64,256]{2,1,0:T(8,128)}), f32[8,64,256]{2,1,0:T(8,128)S(1)}, u32[]{:S(2)}, u32[]{:S(2)}) %all-to-all-start.4) | async-done | bytes 524320 | tf_op jit(solution)/shard_map/all_to_all | solution.py:189
  125.6 0.0 copy-start.3
  125.6 0.8 copy-done.3
  126.4 4.4 %second_sketch.1 = f32[16,8,384]{2,1,0:T(8,128)} custom-call(f32[8,64,256]{2,1,0:T(8,128)} %copy-done.3, f32[256,256]{1,0:T(8,128)} %get-tuple-element.12.x_ref, f32[256,256]{1,0:T(8,128)} %get-tuple-element.14.p_ref, f32[8,8,16,256]{3,2,1,0:T(8,128)} %copy-done.1, f32[8,8,16,256]{3,2,1,0:T(8,128)} %collective-permute-done.4.t_ref), custom_call_target="tpu_custom_call" | custom-call | flops 200000000 | bytes 4000000 | tf_op jit(solution)/shard_map/second_sketch/pallas_call | solution.py:178
  130.9 13.3 %all_to_all.46 = f32[16,8,384]{2,1,0:T(8,128)S(1)} all-to-all(f32[16,8,384]{2,1,0:T(8,128)} %second_sketch.1), channel_id=1, replica_groups=mesh['gx'=16,'gy'=32] {'gx'}, dimensions={0} | all-to-all | bytes 393216 | tf_op jit(solution)/shard_map/all_to_all | solution.py:189
  144.2 0.1 copy.37
  144.3 0.6 copy-done.4
  144.8 0.5 fusion.5
  145.3 20.8 %all_to_all.47 = f32[32,8,384]{2,1,0:T(8,128)S(1)} all-to-all(f32[32,8,384]{2,1,0:T(8,128)S(1)} %fusion.5), channel_id=1, replica_groups=mesh['gx'=16,'gy'=32] {'gy'}, dimensions={0} | all-to-all | bytes 786432 | tf_op jit(solution)/shard_map/all_to_all | solution.py:189
  166.1 0.7 broadcast_in_dim.19
  166.8 0.0 copy-start.6
  166.8 5.7 %all-to-all-start.7 = ((f32[32,8,256]{2,1,0:T(8,128)}), f32[32,8,256]{2,1,0:T(8,128)S(1)}, u32[]{:S(2)}, u32[]{:S(2)}) async-start(f32[32,8,256]{2,1,0:T(8,128)} %broadcast_in_dim.19), calls=%async_computation.7 | async-start | bytes 524288 | tf_op jit(solution)/shard_map/all_to_all | solution.py:189
  172.5 0.0 copy-done.6
  172.5 1.1 fusion.3
  173.6 9.6 %all-to-all-done.7 = f32[32,8,256]{2,1,0:T(8,128)S(1)} async-done(((f32[32,8,256]{2,1,0:T(8,128)}), f32[32,8,256]{2,1,0:T(8,128)S(1)}, u32[]{:S(2)}, u32[]{:S(2)}) %all-to-all-start.7) | async-done | bytes 262176 | tf_op jit(solution)/shard_map/all_to_all | solution.py:189
  183.3 0.7 broadcast_in_dim.20
  184.0 5.6 %all-to-all-start.8 = ((f32[32,8,128]{2,1,0:T(8,128)}), f32[32,8,128]{2,1,0:T(8,128)S(1)}, u32[]{:S(2)}, u32[]{:S(2)}) async-start(f32[32,8,128]{2,1,0:T(8,128)} %broadcast_in_dim.20), calls=%async_computation.8 | async-start | bytes 262144 | tf_op jit(solution)/shard_map/all_to_all | solution.py:189
  189.6 0.0 copy-done.8
  189.6 11.4 %second_factor.1 = (f32[256,256]{1,0:T(8,128)}, f32[128,256]{1,0:T(8,128)}) custom-call(f32[256,256]{1,0:T(8,128)} %bitcast.69, f32[128,384]{1,0:T(8,128)} %bitcast.66), custom_call_target="tpu_custom_call" | custom-call | flops 6000000000 | bytes 786432 | tf_op jit(solution)/shard_map/second_factor/pallas_call | solution.py:166
  200.9 0.0 all-to-all-done.8
  200.9 0.1 copy.38
  201.0 1.3 convolution_bitcast_fusion.2
  202.3 0.6 copy.39
  (13 shorter events, 0.2 us)
Async XLA Ops:
  0.6 1.8 copy-start
  5.0 13.6 %copy-start.9 = (f32[16,8,256]{2,1,0:T(8,128)S(1)}, f32[16,8,256]{2,1,0:T(8,128)}, u32[]{:S(2)}) copy-start(f32[16,8,256]{2,1,0:T(8,128)} %param.5) | copy-start | bytes 393220
  5.0 24.8 %all-to-all-start = ((f32[32,8,256]{2,1,0:T(8,128)}), f32[32,8,256]{2,1,0:T(8,128)S(1)}, u32[]{:S(2)}, u32[]{:S(2)}) async-start(f32[32,8,256]{2,1,0:T(8,128)} %convolution_bitcast_fusion.1), calls=%async_computation | async-start | bytes 524288 | tf_op jit(solution)/shard_map/all_to_all | solution.py:189
  18.7 17.6 %collective-permute-start.1 = (f32[1,8,16,256]{3,2,1,0:T(8,128)S(1)}, f32[1,8,16,256]{3,2,1,0:T(8,128)S(1)}, u32[]{:S(2)}, u32[]{:S(2)}) collective-permute-start(f32[1,8,16,256]{3,2,1,0:T(8,128)S(1)} %bitcast.61), channel_id=1, source_target_pairs={{0,64},{32,480},{64,128},{96,32},{128,192},{160,96},{192,256},{224... | collective-permute-start | bytes 393224 | tf_op jit(solution)/shard_map/ppermute | solution.py:211
  30.6 27.3 %copy-start.2 = (f32[256,128,8]{1,2,0:T(8,128)S(1)}, f32[256,128,8]{1,2,0:T(8,128)}, u32[]{:S(2)}) copy-start(f32[256,128,8]{1,2,0:T(8,128)} %param.3) | copy-start | bytes 3145732
  30.6 27.3 %all-to-all-start.1 = ((f32[32,8,256]{2,1,0:T(8,128)}), f32[32,8,256]{2,1,0:T(8,128)S(1)}, u32[]{:S(2)}, u32[]{:S(2)}) async-start(f32[32,8,256]{2,1,0:T(8,128)} %broadcast_in_dim.14), calls=%async_computation.1 | async-start | bytes 524288 | tf_op jit(solution)/shard_map/all_to_all | solution.py:189
  36.3 11.5 %copy-start.5 = (f32[1,8,16,256]{3,2,1,0:T(8,128)}, f32[1,8,16,256]{3,2,1,0:T(8,128)S(1)}, u32[]{:S(2)}) copy-start(f32[1,8,16,256]{3,2,1,0:T(8,128)S(1)} %collective-permute-done.1) | copy-start | bytes 393220
  36.4 11.4 %collective-permute-start.2 = (f32[2,8,16,256]{3,2,1,0:T(8,128)S(1)}, f32[2,8,16,256]{3,2,1,0:T(8,128)S(1)}, u32[]{:S(2)}, u32[]{:S(2)}) collective-permute-start(f32[2,8,16,256]{3,2,1,0:T(8,128)S(1)} %pad_maximum_fusion.2), channel_id=1, source_target_pairs={{0,128},{32,416},{64,192},{96,480},{128,256},{160,32},{192,320},{2... | collective-permute-start | bytes 786440 | tf_op jit(solution)/shard_map/ppermute | solution.py:211
  47.8 0.7 copy-start.7
  48.5 43.3 %collective-permute-start.3 = (f32[4,8,16,256]{3,2,1,0:T(8,128)S(1)}, f32[4,8,16,256]{3,2,1,0:T(8,128)}, u32[]{:S(2)}, u32[]{:S(2)}) collective-permute-start(f32[4,8,16,256]{3,2,1,0:T(8,128)S(1)} %pad_maximum_fusion.1), channel_id=1, source_target_pairs={{0,256},{32,288},{64,320},{96,352},{128,384},{160,416},{192,448},{... | collective-permute-start | bytes 1572872 | tf_op jit(solution)/shard_map/ppermute | solution.py:211
  60.7 35.4 %collective-permute-start = (f32[8,64,256]{2,1,0:T(8,128)}, f32[8,64,256]{2,1,0:T(8,128)}, u32[]{:S(2)}, u32[]{:S(2)}) collective-permute-start(f32[8,64,256]{2,1,0:T(8,128)} %dynamic-slice_bitcast_fusion), channel_id=1, source_target_pairs={{0,32},{32,0},{64,96},{96,64},{128,160},{160,128},{192,224},{224,1... | collective-permute-start | bytes 1572872 | tf_op jit(solution)/shard_map/ppermute | solution.py:226
  81.9 22.0 %all-to-all-start.3 = ((f32[32,8,256]{2,1,0:T(8,128)}), f32[32,8,256]{2,1,0:T(8,128)}, u32[]{:S(2)}, u32[]{:S(2)}) async-start(f32[32,8,256]{2,1,0:T(8,128)} %broadcast_in_dim.17), calls=%async_computation.3 | async-start | bytes 524288 | tf_op jit(solution)/shard_map/all_to_all | solution.py:189
  93.1 10.9 %copy-start.1 = (f32[8,8,16,256]{3,2,1,0:T(8,128)}, f32[8,8,16,256]{3,2,1,0:T(8,128)S(1)}, u32[]{:S(2)}) copy-start(f32[8,8,16,256]{3,2,1,0:T(8,128)S(1)} %pad_maximum_fusion.s_ref) | copy-start | bytes 3145732
  93.1 27.1 %collective-permute-start.4 = (f32[8,8,16,256]{3,2,1,0:T(8,128)S(1)}, f32[8,8,16,256]{3,2,1,0:T(8,128)}, u32[]{:S(2)}, u32[]{:S(2)}) collective-permute-start(f32[8,8,16,256]{3,2,1,0:T(8,128)S(1)} %pad_maximum_fusion.s_ref), channel_id=1, source_target_pairs={{0,32},{32,0},{64,96},{96,64},{128,160},{160,128},{192,224},{224,1... | collective-permute-start | bytes 3145736 | tf_op jit(solution)/shard_map/ppermute | solution.py:212
  103.9 21.7 %all-to-all-start.4 = ((f32[8,64,256]{2,1,0:T(8,128)}), f32[8,64,256]{2,1,0:T(8,128)S(1)}, u32[]{:S(2)}, u32[]{:S(2)}) async-start(f32[8,64,256]{2,1,0:T(8,128)} %bitcast_add_fusion), calls=%async_computation.4 | async-start | bytes 1048576 | tf_op jit(solution)/shard_map/all_to_all | solution.py:189
  125.6 0.8 copy-start.3
  144.1 0.7 copy-start.4
  166.8 5.7 %copy-start.6 = (f32[256,256]{1,0:T(8,128)S(1)}, f32[256,256]{1,0:T(8,128)}, u32[]{:S(2)}) copy-start(f32[256,256]{1,0:T(8,128)} %get-tuple-element.12.x_ref) | copy-start | bytes 786436
  166.8 16.5 %all-to-all-start.7 = ((f32[32,8,256]{2,1,0:T(8,128)}), f32[32,8,256]{2,1,0:T(8,128)S(1)}, u32[]{:S(2)}, u32[]{:S(2)}) async-start(f32[32,8,256]{2,1,0:T(8,128)} %broadcast_in_dim.19), calls=%async_computation.7 | async-start | bytes 524288 | tf_op jit(solution)/shard_map/all_to_all | solution.py:189
  183.3 6.3 %copy-start.8 = (f32[32,8,256]{2,1,0:T(8,128)}, f32[32,8,256]{2,1,0:T(8,128)S(1)}, u32[]{:S(2)}) copy-start(f32[32,8,256]{2,1,0:T(8,128)S(1)} %all-to-all-done.7) | copy-start | bytes 786436
  184.0 17.0 %all-to-all-start.8 = ((f32[32,8,128]{2,1,0:T(8,128)}), f32[32,8,128]{2,1,0:T(8,128)S(1)}, u32[]{:S(2)}, u32[]{:S(2)}) async-start(f32[32,8,128]{2,1,0:T(8,128)} %broadcast_in_dim.20), calls=%async_computation.8 | async-start | bytes 262144 | tf_op jit(solution)/shard_map/all_to_all | solution.py:189

commit v3 on v2

--- a/solution.py
+++ b/solution.py
@@ -81,7 +81,7 @@
 
 def factor_rows(g_ref, o_ref, d_ref, e_ref, x_ref):
     d_ref[...] = g_ref[:H, :H]
-    e_ref[...] = g_ref[:H, H:]
+    e_ref[...] = g_ref[:H, H : 2 * H]
 
     def body(b, carry):
         eliminate(d_ref, e_ref, x_ref)
@@ -91,7 +91,7 @@
             o_ref[:H, :H] = x_ref[...]
             o_ref[:H, H:] = jnp.zeros((H, H), jnp.float32)
             u = e_ref[...]
-            d_ref[...] = g_ref[H:, H:] - dot0(u, u)
+            d_ref[...] = g_ref[H:, H : 2 * H] - dot0(u, u)
             e_ref[...] = -dot0(u, x_ref[...])
 
         return carry
@@ -108,18 +108,23 @@
     for b in range(16):
         their_y, their_c = b // 2, b % 2
         step = (y - their_y) if their_c == 0 else (their_y - y)
-        place = 8 * (c ^ their_c) + (step & 7)
+        turned = ((step & 1) << 2) | (step & 2) | ((step >> 2) & 1)
+        place = 8 * (c ^ their_c) + turned
         p_ref[pl.ds(pl.multiple_of(16 * place, 16), 16), :] = o_ref[16 * b : 16 * b + 16, :]
 
 
-def second_factor_kernel(g_ref, left_ref, o_ref, b_ref, d_ref, e_ref, x_ref):
+def second_factor_kernel(i_ref, g_ref, left_ref, b_ref, c_ref, o_ref, d_ref, e_ref, x_ref):
     factor_rows(g_ref, o_ref, d_ref, e_ref, x_ref)
     b_ref[...] = dot_t(left_ref[:, :256], o_ref[...])
+    mine = o_ref[pl.ds(pl.multiple_of(8 * i_ref[0], 8), 8), :]
+    core = jnp.dot(mine, g_ref[:, 256:], precision=HI, preferred_element_type=jnp.float32)
+    for k in range(8):
+        c_ref[:, k, :] = core[:, 16 * k : 16 * k + 16]
 
 
 def second_sketch_kernel(m_ref, x_ref, p_ref, s_ref, t_ref, o_ref):
     mixed = m_ref[0]
-    for i in range(1, 8):
+    for i in range(1, 4):
         mixed = mixed + m_ref[i]
     placed = dot_t(mixed, p_ref[...])
     second = jnp.zeros((8, 256), jnp.float32)
@@ -158,20 +163,22 @@
         out_specs=(VMEM, VMEM),
         scratch_shapes=SCRATCH,
         cost_estimate=FACTOR_COST,
+        compiler_params=pltpu.CompilerParams(vmem_limit_bytes=4 << 20),
         name="first_factor",
     )(index, gram)
 
 
-def second_factor(gram, left):
+def second_factor(index, gram, left):
     return pl.pallas_call(
         second_factor_kernel,
-        out_shape=(SQUARE, jax.ShapeDtypeStruct((128, 256), jnp.float32)),
-        in_specs=[VMEM, VMEM],
+        out_shape=(jax.ShapeDtypeStruct((128, 256), jnp.float32), jax.ShapeDtypeStruct((8, 8, 16), jnp.float32)),
+        in_specs=[SMEM, VMEM, VMEM],
         out_specs=(VMEM, VMEM),
-        scratch_shapes=SCRATCH,
+        scratch_shapes=[pltpu.VMEM((256, 256), jnp.float32)] + SCRATCH,
         cost_estimate=FACTOR_COST,
+        compiler_params=pltpu.CompilerParams(vmem_limit_bytes=4 << 20),
         name="second_factor",
-    )(gram, left)
+    )(index, gram, left)
 
 
 def second_sketch(mixed, inverse, placed, near, far):
@@ -181,6 +188,7 @@
         in_specs=[VMEM] * 5,
         out_specs=VMEM,
         cost_estimate=pl.CostEstimate(flops=200_000_000, bytes_accessed=4_000_000, transcendentals=0),
+        compiler_params=pltpu.CompilerParams(vmem_limit_bytes=12 << 20),
         name="second_sketch",
     )(mixed, inverse, placed, near, far)
 
@@ -200,16 +208,14 @@
 def local(tensor, sketch_one, sketch_two):
     gx, gy = 16, 32
     row, col = lax.axis_index("gx"), lax.axis_index("gy")
-    core_of = row % 2
-    twin = [(i, i ^ 1) for i in range(gx)]
 
     def turn(d):
         return [(2 * y + c, 2 * ((y + (d if c == 0 else -d)) % 8) + c) for y in range(8) for c in range(2)]
 
     near = jnp.swapaxes(sketch_two, 0, 1)[None]
-    for d in (1, 2, 4):
+    for d in (4, 2, 1):
         near = jnp.concatenate([near, lax.ppermute(near, "gx", turn(d))], axis=0)
-    far = lax.ppermute(near, "gx", twin)
+    far = lax.ppermute(near, "gx", [(i, i ^ 1) for i in range(gx)])
 
     part = jnp.einsum("ijk,jkc->ic", tensor, sketch_one, precision=HI)
     first_own = sum_scatter(part.reshape(gy, 8, 256), "gy")
@@ -220,12 +226,13 @@
     gram = spread(gram_own, "gy").reshape(256, 256)
 
     mixed_part = jnp.einsum("ijk,ir->kjr", tensor, first, precision=HI)
-    mixed_part = mixed_part.reshape(8, 8, 2, 8, 256).transpose(2, 1, 0, 3, 4).reshape(2, 8, 64, 256)
-    keep = lax.dynamic_index_in_dim(mixed_part, core_of, 0, keepdims=False)
-    give = lax.dynamic_index_in_dim(mixed_part, 1 - core_of, 0, keepdims=False)
-    mixed_half = keep + lax.ppermute(give, "gx", twin)
-    mixed_half, gram = lax.optimization_barrier((mixed_half, gram))
-    mixed = swap(mixed_half, "gx", [list(range(0, gx, 2)), list(range(1, gx, 2))])
+    mixed_part = mixed_part.reshape(8, 4, 2, 2, 8, 256).transpose(3, 2, 1, 0, 4, 5).reshape(2, 2, 4, 64, 256)
+    for bit, here in ((1, row % 2), (2, (row // 2) % 2)):
+        keep = lax.dynamic_index_in_dim(mixed_part, here, 0, keepdims=False)
+        give = lax.dynamic_index_in_dim(mixed_part, 1 - here, 0, keepdims=False)
+        mixed_part = keep + lax.ppermute(give, "gx", [(i, i ^ bit) for i in range(gx)])
+    mixed_part, gram = lax.optimization_barrier((mixed_part, gram))
+    mixed = swap(mixed_part, "gx", [list(range(i, gx, 4)) for i in range(4)])
 
     inv_one, placed = first_factor(row.astype(jnp.int32)[None], gram)
     basis_one = jnp.einsum("it,st->is", first, inv_one, precision=HI)
@@ -234,12 +241,8 @@
 
     both_part = lax.dot_general(left[:, :256], left, (((0,), (0,)), ((), ())), precision=HI)
     both_own = sum_scatter(both_part.reshape(gy, 8, 384), "gy")
-    gram_two = spread(both_own[:, :256], "gy").reshape(256, 256)
-    core_own, gram_two = lax.optimization_barrier((both_own[:, 256:], gram_two))
-    core_in = spread(core_own, "gy").reshape(256, 128)
-    inv_two, basis_two = second_factor(gram_two, left)
-    mine = lax.dynamic_slice_in_dim(inv_two, 8 * col, 8, 0)
-    core = jnp.dot(mine, core_in, precision=HI).reshape(8, 8, 16)
+    both = spread(both_own, "gy").reshape(256, 384)
+    basis_two, core = second_factor(col.astype(jnp.int32)[None], both, left)
     return (basis_one, basis_two, jnp.transpose(core, (2, 0, 1)))
 
 

time: 204 us -> 190 us (0.931)
  starting transfers between devices: 67.9 us -> 53.3 us
  blocking collectives: 52 us -> 65.9 us
  waiting for transfers between devices: 35.6 us -> 25.8 us
  Pallas kernels: 26.8 us -> 22.6 us
    all_to_all x6 -> x5, starting transfers between devices: 45.6 us -> 30.7 us  [swap(): lax.all_to_all(pieces, axis, 0, 0, axis_index_groups=groups, tiled=True)]
    all_to_all x3, blocking collectives: 52 us -> 65.9 us  [swap(): lax.all_to_all(pieces, axis, 0, 0, axis_index_groups=groups, tiled=True)]
    all_to_all x6 -> x5, waiting for transfers between devices: 28.6 us -> 16.4 us  [swap(): lax.all_to_all(pieces, axis, 0, 0, axis_index_groups=groups, tiled=True)]
    ppermute x2 -> x3, waiting for transfers between devices: 0.01 us -> 4.84 us  [the longest x2 4.84 us: local(): lax.ppermute(give, 'gx', [(i, i ^ bit) for i in range(gx)])]
    ppermute x3, waiting for transfers between devices: 6.92 us -> 4.56 us  [local(): near = jnp.concatenate([near, lax.ppermute(near, 'gx', turn(d))], axis=0)]
    ppermute x2 -> x3, starting transfers between devices: 4.94 us -> 6.39 us  [the longest x2 4.47 us: local(): lax.ppermute(give, 'gx', [(i, i ^ bit) for i in range(gx)])]
    unnamed x23 -> x22, local copies, waits for them, and re-layouts: 4.56 us -> 5.2 us
  transfers between devices with their start and end apart: 11 -> 11, of which waited for: 5 -> 4; matrix products, arithmetic and copies ran while one was open for 5% -> 6% of each run, Pallas kernels for 11% -> 5%
where the time goes in v3:
time: 190 us; the launch traced here: 189 us
  blocking collectives  65.9 us (35%)
  starting transfers between devices  53.3 us (28%)
  waiting for transfers between devices  25.8 us (14%)
  Pallas kernels  22.6 us (12%)
  local copies, waits for them, and re-layouts  9.97 us (5%)
  matrix products  5.82 us (3%)
  other arithmetic  4.98 us (3%)
    all_to_all x3, blocking collectives, swap(): lax.all_to_all(pieces, axis, 0, 0, axis_index_groups=groups, tiled=True)  65.9 us
    all_to_all x5, starting transfers between devices, swap(): lax.all_to_all(pieces, axis, 0, 0, axis_index_groups=groups, tiled=True)  30.7 us
    all_to_all x5, waiting for transfers between devices, swap(): lax.all_to_all(pieces, axis, 0, 0, axis_index_groups=groups, tiled=True)  16.4 us
    ppermute x3, starting transfers between devices, local(): near = jnp.concatenate([near, lax.ppermute(near, 'gx', turn(d))], axis=0)  16.2 us
    pallas_call x1, Pallas kernels, second_factor(): pl.pallas_call(second_factor_kernel, out_shape=(jax.ShapeDtypeStruct((128...  10.4 us
    pallas_call x1, Pallas kernels, first_factor(): pl.pallas_call(first_factor_kernel, out_shape=(SQUARE, SQUARE), in_specs=...  9.34 us
    unnamed x22, local copies, waits for them, and re-layouts  5.2 us
    ppermute x2, waiting for transfers between devices, local(): lax.ppermute(give, 'gx', [(i, i ^ bit) for i in range(gx)])  4.84 us
  transfers between devices with their start and end apart: 11, of which 4 were waited for; matrix products, arithmetic and copies ran while one was open for 6% of the time, Pallas kernels for 5%

profile of v3, /device:TPU:2, one launch (start us, length us, event | category | flops | bytes accessed | tf_op | source)
XLA Modules:
  0.0 189.4 jit_solution(9748848084693007878)
XLA Ops:
  0.6 0.0 copy-start
  0.6 1.8 copy.26
  2.5 0.0 copy-done
  2.5 1.8 convolution_bitcast_fusion.1
  4.3 0.0 copy-start.9
  4.3 24.6 %all_to_all.40 = f32[32,8,256]{2,1,0:T(8,128)S(1)} all-to-all(f32[32,8,256]{2,1,0:T(8,128)S(1)} %convolution_bitcast_fusion.1), channel_id=1, replica_groups=mesh['gx'=16,'gy'=32] {'gy'}, dimensions={0} | all-to-all | bytes 524288 | tf_op jit(solution)/shard_map/all_to_all | solution.py:197
  28.9 0.0 copy-start.5
  29.0 0.7 broadcast_in_dim.14
  29.7 5.6 %all-to-all-start.1 = ((f32[32,8,256]{2,1,0:T(8,128)}), f32[32,8,256]{2,1,0:T(8,128)S(1)}, u32[]{:S(2)}, u32[]{:S(2)}) async-start(f32[32,8,256]{2,1,0:T(8,128)} %broadcast_in_dim.14), calls=%async_computation.1 | async-start | bytes 524288 | tf_op jit(solution)/shard_map/all_to_all | solution.py:197
  35.3 0.0 copy-done.9
  35.3 7.7 %collective-permute-start.2 = (f32[1,8,16,256]{3,2,1,0:T(8,128)S(1)}, f32[1,8,16,256]{3,2,1,0:T(8,128)S(1)}, u32[]{:S(2)}, u32[]{:S(2)}) collective-permute-start(f32[1,8,16,256]{3,2,1,0:T(8,128)S(1)} %bitcast.61), channel_id=1, source_target_pairs={{0,256},{32,288},{64,320},{96,352},{128,384},{160,416},{192,448},{... | collective-permute-start | bytes 393224 | tf_op jit(solution)/shard_map/ppermute | solution.py:217
  43.1 4.6 %collective-permute-done.2 = f32[1,8,16,256]{3,2,1,0:T(8,128)S(1)} collective-permute-done((f32[1,8,16,256]{3,2,1,0:T(8,128)S(1)}, f32[1,8,16,256]{3,2,1,0:T(8,128)S(1)}, u32[]{:S(2)}, u32[]{:S(2)}) %collective-permute-start.2) | collective-permute-done | bytes 131104 | tf_op jit(solution)/shard_map/ppermute | solution.py:217
  47.7 4.7 %collective-permute-start.3 = (f32[2,8,16,256]{3,2,1,0:T(8,128)S(1)}, f32[2,8,16,256]{3,2,1,0:T(8,128)S(1)}, u32[]{:S(2)}, u32[]{:S(2)}) collective-permute-start(f32[2,8,16,256]{3,2,1,0:T(8,128)S(1)} %pad_maximum_fusion.2), channel_id=1, source_target_pairs={{0,128},{32,416},{64,192},{96,480},{128,256},{160,32},{192,320},{2... | collective-permute-start | bytes 786440 | tf_op jit(solution)/shard_map/ppermute | solution.py:217
  52.4 0.0 all-to-all-done.1
  52.4 0.0 copy-done.5
  52.4 0.0 copy-start.6
  52.4 1.8 fusion
  54.2 0.1 copy.35
  54.3 0.9 dynamic-slice_bitcast_fusion
  55.2 1.9 %collective-permute-start = (f32[2,4,64,256]{3,2,1,0:T(8,128)}, f32[2,4,64,256]{3,2,1,0:T(8,128)}, u32[]{:S(2)}, u32[]{:S(2)}) collective-permute-start(f32[2,4,64,256]{3,2,1,0:T(8,128)} %dynamic-slice_bitcast_fusion), channel_id=1, source_target_pairs={{0,32},{32,0},{64,96},{96,64},{128,160},{160,128},{192,224},{224,1... | collective-permute-start | bytes 1572872 | tf_op jit(solution)/shard_map/ppermute | solution.py:233
  57.1 0.0 copy-done.6
  57.1 0.6 convolution_bitcast_fusion
  57.8 0.7 broadcast_in_dim.16
  58.4 5.4 %all-to-all-start.2 = ((f32[16,8,256]{2,1,0:T(8,128)}), f32[16,8,256]{2,1,0:T(8,128)S(1)}, u32[]{:S(2)}, u32[]{:S(2)}) async-start(f32[16,8,256]{2,1,0:T(8,128)} %broadcast_in_dim.16), calls=%async_computation.2 | async-start | bytes 262144 | tf_op jit(solution)/shard_map/all_to_all | solution.py:197
  63.9 0.0 collective-permute-done.3
  63.9 0.8 pad_maximum_fusion.1
  64.7 3.8 %collective-permute-start.4 = (f32[4,8,16,256]{3,2,1,0:T(8,128)}, f32[4,8,16,256]{3,2,1,0:T(8,128)}, u32[]{:S(2)}, u32[]{:S(2)}) collective-permute-start(f32[4,8,16,256]{3,2,1,0:T(8,128)} %pad_maximum_fusion.1), channel_id=1, source_target_pairs={{0,64},{32,480},{64,128},{96,32},{128,192},{160,96},{192,256},{224... | collective-permute-start | bytes 1572872 | tf_op jit(solution)/shard_map/ppermute | solution.py:217
  68.6 3.9 %all-to-all-done.2 = f32[16,8,256]{2,1,0:T(8,128)S(1)} async-done(((f32[16,8,256]{2,1,0:T(8,128)}), f32[16,8,256]{2,1,0:T(8,128)S(1)}, u32[]{:S(2)}, u32[]{:S(2)}) %all-to-all-start.2) | async-done | bytes 131104 | tf_op jit(solution)/shard_map/all_to_all | solution.py:197
  72.5 0.7 broadcast_in_dim.17
  73.3 9.8 %all-to-all-start.3 = ((f32[32,8,256]{2,1,0:T(8,128)}), f32[32,8,256]{2,1,0:T(8,128)S(1)}, u32[]{:S(2)}, u32[]{:S(2)}) async-start(f32[32,8,256]{2,1,0:T(8,128)} %broadcast_in_dim.17), calls=%async_computation.3 | async-start | bytes 524288 | tf_op jit(solution)/shard_map/all_to_all | solution.py:197
  83.0 0.0 collective-permute-done
  83.1 1.1 bitcast_add_fusion
  84.2 0.0 copy-start.8
  84.2 0.8 dynamic-slice_bitcast_fusion.1
  85.0 2.6 %collective-permute-start.1 = (f32[4,64,256]{2,1,0:T(8,128)}, f32[4,64,256]{2,1,0:T(8,128)}, u32[]{:S(2)}, u32[]{:S(2)}) collective-permute-start(f32[4,64,256]{2,1,0:T(8,128)} %dynamic-slice_bitcast_fusion.1), channel_id=1, source_target_pairs={{0,64},{32,96},{64,0},{96,32},{128,192},{160,224},{192,128},{224,1... | collective-permute-start | bytes 786440 | tf_op jit(solution)/shard_map/ppermute | solution.py:233
  87.6 0.0 collective-permute-done.4
  87.6 0.0 copy-done.8
  87.6 1.1 pad_maximum_fusion.s_ref
  88.7 1.9 %collective-permute-start.5 = (f32[8,8,16,256]{3,2,1,0:T(8,128)S(1)}, f32[8,8,16,256]{3,2,1,0:T(8,128)S(1)}, u32[]{:S(2)}, u32[]{:S(2)}) collective-permute-start(f32[8,8,16,256]{3,2,1,0:T(8,128)S(1)} %pad_maximum_fusion.s_ref), channel_id=1, source_target_pairs={{0,32},{32,0},{64,96},{96,64},{128,160},{160,128},{192,224},{224,1... | collective-permute-start | bytes 3145736 | tf_op jit(solution)/shard_map/ppermute | solution.py:218
  90.7 4.8 %collective-permute-done.1 = f32[4,64,256]{2,1,0:T(8,128)} collective-permute-done((f32[4,64,256]{2,1,0:T(8,128)}, f32[4,64,256]{2,1,0:T(8,128)}, u32[]{:S(2)}, u32[]{:S(2)}) %collective-permute-start.1) | collective-permute-done | bytes 262176 | tf_op jit(solution)/shard_map/ppermute | solution.py:233
  95.5 1.8 bitcast_add_fusion.1
  97.3 0.0 all-to-all-done.3
  97.3 0.0 copy-start.3
  97.3 0.7 copy-done.3
  98.0 4.2 %all-to-all-start.4 = ((f32[4,64,256]{2,1,0:T(8,128)}), f32[4,64,256]{2,1,0:T(8,128)}, u32[]{:S(2)}, u32[]{:S(2)}) async-start(f32[4,64,256]{2,1,0:T(8,128)} %bitcast_add_fusion.1), calls=%async_computation.4 | async-start | bytes 524288 | tf_op jit(solution)/shard_map/all_to_all | solution.py:197
  102.2 0.0 copy-start.4
  102.2 0.9 copy-done.4
  103.2 9.3 %first_factor.1 = (f32[256,256]{1,0:T(8,128)S(1)}, f32[256,256]{1,0:T(8,128)S(1)}) custom-call(s32[1]{0:T(128)} %bitcast.3.i_ref, f32[256,256]{1,0:T(8,128)S(1)} %bitcast.57), custom_call_target="tpu_custom_call" | custom-call | flops 6000000000 | bytes 786432 | tf_op jit(solution)/shard_map/first_factor/pallas_call | solution.py:159
  112.5 0.0 copy-start.1
  112.5 0.7 copy-done.1
  113.2 0.0 collective-permute-done.5.t_ref
  113.2 0.0 all-to-all-done.4.m_ref
  113.3 0.9 copy-done.2
  114.2 2.8 %second_sketch.1 = f32[16,8,384]{2,1,0:T(8,128)S(1)} custom-call(f32[4,64,256]{2,1,0:T(8,128)} %all-to-all-done.4.m_ref, f32[256,256]{1,0:T(8,128)S(1)} %get-tuple-element.10.x_ref, f32[256,256]{1,0:T(8,128)S(1)} %copy-done.2, f32[8,8,16,256]{3,2,1,0:T(8,128)S(1)} %pad_maximum_fusion.s_ref, f32[8,8,16,256]{3,2,1,0:T(8,128)S(1)} %collective-permute-done.5.t_ref), custom_call_target="tpu_custom_call" | custom-call | flops 200000000 | bytes 4000000 | tf_op jit(solution)/shard_map/second_sketch/pallas_call | solution.py:185
  117.0 16.8 %all_to_all.41 = f32[16,8,384]{2,1,0:T(8,128)S(1)} all-to-all(f32[16,8,384]{2,1,0:T(8,128)S(1)} %second_sketch.1), channel_id=1, replica_groups=mesh['gx'=16,'gy'=32] {'gx'}, dimensions={0} | all-to-all | bytes 393216 | tf_op jit(solution)/shard_map/all_to_all | solution.py:197
  133.8 0.1 copy.30
  133.9 0.5 fusion.5
  134.4 24.5 %all_to_all.42 = f32[32,8,384]{2,1,0:T(8,128)S(1)} all-to-all(f32[32,8,384]{2,1,0:T(8,128)S(1)} %fusion.5), channel_id=1, replica_groups=mesh['gx'=16,'gy'=32] {'gy'}, dimensions={0} | all-to-all | bytes 786432 | tf_op jit(solution)/shard_map/all_to_all | solution.py:197
  158.9 0.8 broadcast_in_dim.39
  159.7 5.7 %all-to-all-start.7 = ((f32[32,8,384]{2,1,0:T(8,128)}), f32[32,8,384]{2,1,0:T(8,128)S(1)}, u32[]{:S(2)}, u32[]{:S(2)}) async-start(f32[32,8,384]{2,1,0:T(8,128)} %broadcast_in_dim.39), calls=%async_computation.7 | async-start | bytes 786432 | tf_op jit(solution)/shard_map/all_to_all | solution.py:197
  165.4 0.0 copy-done.7
  165.4 1.1 fusion.3
  166.5 12.4 %all-to-all-done.7 = f32[32,8,384]{2,1,0:T(8,128)S(1)} async-done(((f32[32,8,384]{2,1,0:T(8,128)}), f32[32,8,384]{2,1,0:T(8,128)S(1)}, u32[]{:S(2)}, u32[]{:S(2)}) %all-to-all-start.7) | async-done | bytes 393248 | tf_op jit(solution)/shard_map/all_to_all | solution.py:197
  179.0 10.4 %second_factor.1 = (f32[128,256]{1,0:T(8,128)}, f32[8,8,16]{2,1,0:T(8,128)}) custom-call(s32[1]{0:T(128)} %bitcast.16.i_ref, f32[256,384]{1,0:T(8,128)S(1)} %bitcast.56, f32[128,384]{1,0:T(8,128)S(1)} %bitcast.55), custom_call_target="tpu_custom_call" | custom-call | flops 6000000000 | bytes 786432 | tf_op jit(solution)/shard_map/second_factor/pallas_call | solution.py:172
  (9 shorter events, 0.2 us)
Async XLA Ops:
  0.6 1.8 copy-start
  4.3 31.0 %copy-start.9 = (f32[16,8,256]{2,1,0:T(8,128)S(1)}, f32[16,8,256]{2,1,0:T(8,128)}, u32[]{:S(2)}) copy-start(f32[16,8,256]{2,1,0:T(8,128)} %param.5) | copy-start | bytes 393220
  28.9 23.4 %copy-start.5 = (f32[256,128,8]{1,2,0:T(8,128)S(1)}, f32[256,128,8]{1,2,0:T(8,128)}, u32[]{:S(2)}) copy-start(f32[256,128,8]{1,2,0:T(8,128)} %param.3) | copy-start | bytes 3145732
  29.7 22.7 %all-to-all-start.1 = ((f32[32,8,256]{2,1,0:T(8,128)}), f32[32,8,256]{2,1,0:T(8,128)S(1)}, u32[]{:S(2)}, u32[]{:S(2)}) async-start(f32[32,8,256]{2,1,0:T(8,128)} %broadcast_in_dim.14), calls=%async_computation.1 | async-start | bytes 524288 | tf_op jit(solution)/shard_map/all_to_all | solution.py:197
  35.3 12.3 %collective-permute-start.2 = (f32[1,8,16,256]{3,2,1,0:T(8,128)S(1)}, f32[1,8,16,256]{3,2,1,0:T(8,128)S(1)}, u32[]{:S(2)}, u32[]{:S(2)}) collective-permute-start(f32[1,8,16,256]{3,2,1,0:T(8,128)S(1)} %bitcast.61), channel_id=1, source_target_pairs={{0,256},{32,288},{64,320},{96,352},{128,384},{160,416},{192,448},{... | collective-permute-start | bytes 393224 | tf_op jit(solution)/shard_map/ppermute | solution.py:217
  47.7 16.2 %collective-permute-start.3 = (f32[2,8,16,256]{3,2,1,0:T(8,128)S(1)}, f32[2,8,16,256]{3,2,1,0:T(8,128)S(1)}, u32[]{:S(2)}, u32[]{:S(2)}) collective-permute-start(f32[2,8,16,256]{3,2,1,0:T(8,128)S(1)} %pad_maximum_fusion.2), channel_id=1, source_target_pairs={{0,128},{32,416},{64,192},{96,480},{128,256},{160,32},{192,320},{2... | collective-permute-start | bytes 786440 | tf_op jit(solution)/shard_map/ppermute | solution.py:217
  52.4 4.7 %copy-start.6 = (f32[32,8,256]{2,1,0:T(8,128)}, f32[32,8,256]{2,1,0:T(8,128)S(1)}, u32[]{:S(2)}) copy-start(f32[32,8,256]{2,1,0:T(8,128)S(1)} %all-to-all-done.1) | copy-start | bytes 786436
  55.2 27.8 %collective-permute-start = (f32[2,4,64,256]{3,2,1,0:T(8,128)}, f32[2,4,64,256]{3,2,1,0:T(8,128)}, u32[]{:S(2)}, u32[]{:S(2)}) collective-permute-start(f32[2,4,64,256]{3,2,1,0:T(8,128)} %dynamic-slice_bitcast_fusion), channel_id=1, source_target_pairs={{0,32},{32,0},{64,96},{96,64},{128,160},{160,128},{192,224},{224,1... | collective-permute-start | bytes 1572872 | tf_op jit(solution)/shard_map/ppermute | solution.py:233
  58.4 14.1 %all-to-all-start.2 = ((f32[16,8,256]{2,1,0:T(8,128)}), f32[16,8,256]{2,1,0:T(8,128)S(1)}, u32[]{:S(2)}, u32[]{:S(2)}) async-start(f32[16,8,256]{2,1,0:T(8,128)} %broadcast_in_dim.16), calls=%async_computation.2 | async-start | bytes 262144 | tf_op jit(solution)/shard_map/all_to_all | solution.py:197
  64.7 22.9 %collective-permute-start.4 = (f32[4,8,16,256]{3,2,1,0:T(8,128)}, f32[4,8,16,256]{3,2,1,0:T(8,128)}, u32[]{:S(2)}, u32[]{:S(2)}) collective-permute-start(f32[4,8,16,256]{3,2,1,0:T(8,128)} %pad_maximum_fusion.1), channel_id=1, source_target_pairs={{0,64},{32,480},{64,128},{96,32},{128,192},{160,96},{192,256},{224... | collective-permute-start | bytes 1572872 | tf_op jit(solution)/shard_map/ppermute | solution.py:217
  73.3 24.0 %all-to-all-start.3 = ((f32[32,8,256]{2,1,0:T(8,128)}), f32[32,8,256]{2,1,0:T(8,128)S(1)}, u32[]{:S(2)}, u32[]{:S(2)}) async-start(f32[32,8,256]{2,1,0:T(8,128)} %broadcast_in_dim.17), calls=%async_computation.3 | async-start | bytes 524288 | tf_op jit(solution)/shard_map/all_to_all | solution.py:197
  84.2 3.4 %copy-start.8 = (f32[2,4,64,256]{3,2,1,0:T(8,128)}, f32[2,4,64,256]{3,2,1,0:T(8,128)S(1)}, u32[]{:S(2)}) copy-start(f32[2,4,64,256]{3,2,1,0:T(8,128)S(1)} %bitcast_add_fusion) | copy-start | bytes 1572868
  85.0 10.5 %collective-permute-start.1 = (f32[4,64,256]{2,1,0:T(8,128)}, f32[4,64,256]{2,1,0:T(8,128)}, u32[]{:S(2)}, u32[]{:S(2)}) collective-permute-start(f32[4,64,256]{2,1,0:T(8,128)} %dynamic-slice_bitcast_fusion.1), channel_id=1, source_target_pairs={{0,64},{32,96},{64,0},{96,32},{128,192},{160,224},{192,128},{224,1... | collective-permute-start | bytes 786440 | tf_op jit(solution)/shard_map/ppermute | solution.py:233
  88.7 24.5 %collective-permute-start.5 = (f32[8,8,16,256]{3,2,1,0:T(8,128)S(1)}, f32[8,8,16,256]{3,2,1,0:T(8,128)S(1)}, u32[]{:S(2)}, u32[]{:S(2)}) collective-permute-start(f32[8,8,16,256]{3,2,1,0:T(8,128)S(1)} %pad_maximum_fusion.s_ref), channel_id=1, source_target_pairs={{0,32},{32,0},{64,96},{96,64},{128,160},{160,128},{192,224},{224,1... | collective-permute-start | bytes 3145736 | tf_op jit(solution)/shard_map/ppermute | solution.py:218
  97.3 0.7 copy-start.3
  98.0 15.3 %all-to-all-start.4 = ((f32[4,64,256]{2,1,0:T(8,128)}), f32[4,64,256]{2,1,0:T(8,128)}, u32[]{:S(2)}, u32[]{:S(2)}) async-start(f32[4,64,256]{2,1,0:T(8,128)} %bitcast_add_fusion.1), calls=%async_computation.4 | async-start | bytes 524288 | tf_op jit(solution)/shard_map/all_to_all | solution.py:197
  102.2 1.0 copy-start.4
  112.5 0.7 copy-start.1
  113.2 1.0 copy-start.2
  159.7 5.7 %copy-start.7 = (f32[32,8,256]{2,1,0:T(8,128)S(1)}, f32[32,8,256]{2,1,0:T(8,128)}, u32[]{:S(2)}) copy-start(f32[32,8,256]{2,1,0:T(8,128)} %copy-done.6) | copy-start | bytes 786436
  159.7 19.3 %all-to-all-start.7 = ((f32[32,8,384]{2,1,0:T(8,128)}), f32[32,8,384]{2,1,0:T(8,128)S(1)}, u32[]{:S(2)}, u32[]{:S(2)}) async-start(f32[32,8,384]{2,1,0:T(8,128)} %broadcast_in_dim.39), calls=%async_computation.7 | async-start | bytes 786432 | tf_op jit(solution)/shard_map/all_to_all | solution.py:197

commit v4 on v3

--- a/solution.py
+++ b/solution.py
@@ -20,6 +20,7 @@
 def eliminate(d_ref,e_ref,x_ref):
     sub=lax.broadcasted_iota(jnp.int32,(8,H),0)
     lane=lax.broadcasted_iota(jnp.int32,(8,H),1)
+    left=[]; right=[]
     for k in range(16):
         rows=slice(8*k,8*k+8)
         block=(lane>=8*k)&(lane<8*k+8)
@@ -50,7 +51,7 @@
             for t in range(q):
                 uD[q]=uD[q]+W[q][t]*rD[t]
                 uE[q]=uE[q]+W[q][t]*rE[t]
-        for g in range(k+1,16):
+        for g in range(k+1,min(16,(k//8+1)*8)):
             gr=slice(8*g,8*g+8)
             Dg=d_ref[gr,:]; Eg=e_ref[gr,:]
             c=[spread_col(Dg,8*k+t) for t in range(8)]
@@ -63,12 +64,23 @@
                 Dg=Dg-a*uD[j]; Eg=Eg-a*uE[j]
             d_ref[gr,:]=Dg; e_ref[gr,:]=Eg
         rs=1.0/jnp.sqrt(dsel)
-        nD=uD[0]; nE=uE[0]
+        nD=uD[0]; nE=uE[0]; isel=inv[0]
         for q in range(1,8):
-            nD=jnp.where(sub==q,uD[q],nD); nE=jnp.where(sub==q,uE[q],nE)
+            nD=jnp.where(sub==q,uD[q],nD); nE=jnp.where(sub==q,uE[q],nE); isel=jnp.where(sub==q,inv[q],isel)
         row=8*k+sub
         x_ref[rows,:]=jnp.where(lane<=row,nD,0.0)*rs
         e_ref[rows,:]=nE*rs
+        end=8*8*(k//8+1)
+        left.append(nD*isel)
+        right.append(jnp.concatenate([jnp.where((lane<=row)|(lane>=end),nD,0.0),nE],axis=1))
+        if k%8==8-1 and k<15:
+            upd=dot0(jnp.concatenate(left,axis=0),jnp.concatenate(right,axis=0))
+            left=[]; right=[]
+            inblk=(lane>=end-8*8)&(lane<end)
+            for g in range(k+1,16):
+                gr=slice(8*g,8*g+8)
+                d_ref[gr,:]=jnp.where(inblk,0.0,d_ref[gr,:])-upd[gr,:H]
+                e_ref[gr,:]=e_ref[gr,:]-upd[gr,H:]
 
 
 def dot0(a,b):
@@ -99,6 +111,15 @@
     lax.fori_loop(0, 2, body, 0)
     o_ref[H:, H:] = x_ref[...]
     o_ref[H:, :H] = e_ref[...]
+
+
+def first_dot_kernel(a_ref, s_ref, o_ref):
+    total = jnp.zeros((256, 256), jnp.float32)
+    for k in range(0, 8, 2):
+        cells = jnp.concatenate([a_ref[:, k, :], a_ref[:, k + 1, :]], axis=1)
+        test = jnp.concatenate([s_ref[:, k, :], s_ref[:, k + 1, :]], axis=0)
+        total = total + jnp.dot(cells, test, precision=HI, preferred_element_type=jnp.float32)
+    o_ref[...] = total
 
 
 def first_factor_kernel(i_ref, g_ref, o_ref, p_ref, d_ref, e_ref, x_ref):
@@ -148,11 +169,24 @@
         o_ref[m, :, 256:] = chunk
 
 
+GRANT = 5 << 20
 VMEM = pl.BlockSpec(memory_space=pltpu.VMEM)
 SMEM = pl.BlockSpec(memory_space=pltpu.SMEM)
 SQUARE = jax.ShapeDtypeStruct((256, 256), jnp.float32)
 SCRATCH = [pltpu.VMEM((H, H), jnp.float32)] * 3
 FACTOR_COST = pl.CostEstimate(flops=6_000_000_000, bytes_accessed=786432, transcendentals=0)
+
+
+def first_dot(cells, test):
+    return pl.pallas_call(
+        first_dot_kernel,
+        out_shape=SQUARE,
+        in_specs=[VMEM, VMEM],
+        out_specs=VMEM,
+        cost_estimate=pl.CostEstimate(flops=800_000_000, bytes_accessed=2_500_000, transcendentals=0),
+        compiler_params=pltpu.CompilerParams(vmem_limit_bytes=GRANT),
+        name="first_dot",
+    )(cells, test)
 
 
 def first_factor(index, gram):
@@ -163,7 +197,7 @@
         out_specs=(VMEM, VMEM),
         scratch_shapes=SCRATCH,
         cost_estimate=FACTOR_COST,
-        compiler_params=pltpu.CompilerParams(vmem_limit_bytes=4 << 20),
+        compiler_params=pltpu.CompilerParams(vmem_limit_bytes=GRANT),
         name="first_factor",
     )(index, gram)
 
@@ -176,7 +210,7 @@
         out_specs=(VMEM, VMEM),
         scratch_shapes=[pltpu.VMEM((256, 256), jnp.float32)] + SCRATCH,
         cost_estimate=FACTOR_COST,
-        compiler_params=pltpu.CompilerParams(vmem_limit_bytes=4 << 20),
+        compiler_params=pltpu.CompilerParams(vmem_limit_bytes=GRANT),
         name="second_factor",
     )(index, gram, left)
 
@@ -188,7 +222,7 @@
         in_specs=[VMEM] * 5,
         out_specs=VMEM,
         cost_estimate=pl.CostEstimate(flops=200_000_000, bytes_accessed=4_000_000, transcendentals=0),
-        compiler_params=pltpu.CompilerParams(vmem_limit_bytes=12 << 20),
+        compiler_params=pltpu.CompilerParams(vmem_limit_bytes=GRANT),
         name="second_sketch",
     )(mixed, inverse, placed, near, far)
 
@@ -217,7 +251,7 @@
         near = jnp.concatenate([near, lax.ppermute(near, "gx", turn(d))], axis=0)
     far = lax.ppermute(near, "gx", [(i, i ^ 1) for i in range(gx)])
 
-    part = jnp.einsum("ijk,jkc->ic", tensor, sketch_one, precision=HI)
+    part = first_dot(jnp.swapaxes(tensor, 1, 2), sketch_one)
     first_own = sum_scatter(part.reshape(gy, 8, 256), "gy")
     first = spread(first_own, "gy").reshape(256, 256)
 
@@ -231,7 +265,6 @@
         keep = lax.dynamic_index_in_dim(mixed_part, here, 0, keepdims=False)
         give = lax.dynamic_index_in_dim(mixed_part, 1 - here, 0, keepdims=False)
         mixed_part = keep + lax.ppermute(give, "gx", [(i, i ^ bit) for i in range(gx)])
-    mixed_part, gram = lax.optimization_barrier((mixed_part, gram))
     mixed = swap(mixed_part, "gx", [list(range(i, gx, 4)) for i in range(4)])
 
     inv_one, placed = first_factor(row.astype(jnp.int32)[None], gram)

time: 190 us -> 183 us (0.963)
  local copies, waits for them, and re-layouts: 9.97 us -> 6.35 us
    unnamed x22 -> x9, local copies, waits for them, and re-layouts: 5.2 us -> 2.5 us
    pallas_call x0 -> x1, Pallas kernels: none -> 1.91 us  [first_dot(): pl.pallas_call(first_dot_kernel, out_shape=SQUARE, in_specs=[VMEM, VMEM],...]
  transfers between devices with their start and end apart: 11 -> 11, of which waited for: 4 -> 5; matrix products, arithmetic and copies ran while one was open for 6% -> 5% of each run, Pallas kernels for 5% -> 5%
where the time goes in v4:
time: 183 us; the launch traced here: 182 us
  blocking collectives  65 us (36%)
  starting transfers between devices  52.6 us (29%)
  waiting for transfers between devices  26.6 us (15%)
  Pallas kernels  23.1 us (13%)
  local copies, waits for them, and re-layouts  6.35 us (3%)
  matrix products  4 us (2%)
  other arithmetic  3.84 us (2%)
    all_to_all x3, blocking collectives, swap(): lax.all_to_all(pieces, axis, 0, 0, axis_index_groups=groups, tiled=True)  65 us
    all_to_all x5, starting transfers between devices, swap(): lax.all_to_all(pieces, axis, 0, 0, axis_index_groups=groups, tiled=True)  29.9 us
    all_to_all x5, waiting for transfers between devices, swap(): lax.all_to_all(pieces, axis, 0, 0, axis_index_groups=groups, tiled=True)  17.2 us
    ppermute x3, starting transfers between devices, local(): near = jnp.concatenate([near, lax.ppermute(near, 'gx', turn(d))], axis=0)  16.2 us
    pallas_call x1, Pallas kernels, second_factor(): pl.pallas_call(second_factor_kernel, out_shape=(jax.ShapeDtypeStruct((128...  10.2 us
    pallas_call x1, Pallas kernels, first_factor(): pl.pallas_call(first_factor_kernel, out_shape=(SQUARE, SQUARE), in_specs=...  9.08 us
    ppermute x2, waiting for transfers between devices, local(): lax.ppermute(give, 'gx', [(i, i ^ bit) for i in range(gx)])  4.84 us
    ppermute x3, waiting for transfers between devices, local(): near = jnp.concatenate([near, lax.ppermute(near, 'gx', turn(d))], axis=0)  4.57 us
  transfers between devices with their start and end apart: 11, of which 5 were waited for; matrix products, arithmetic and copies ran while one was open for 5% of the time, Pallas kernels for 5%

profile of v4, /device:TPU:2, one launch (start us, length us, event | category | flops | bytes accessed | tf_op | source)
XLA Modules:
  0.0 182.5 jit_solution(1870053196926441001)
XLA Ops:
  0.6 0.0 copy-start
  0.6 1.2 copy-done
  1.9 0.0 copy-start.2
  1.9 1.2 copy-done.2
  3.1 1.9 %first_dot.1 = f32[256,256]{1,0:T(8,128)S(1)} custom-call(f32[256,8,128]{2,1,0:T(8,128)S(1)} %bitcast.52, f32[128,8,256]{2,1,0:T(8,128)S(1)} %copy-done.2), custom_call_target="tpu_custom_call" | custom-call | flops 800000000 | bytes 2500000 | tf_op jit(solution)/shard_map/first_dot/pallas_call | solution.py:181
  5.0 0.0 copy-start.3
  5.0 24.6 %all_to_all.40 = f32[32,8,256]{2,1,0:T(8,128)S(1)} all-to-all(f32[32,8,256]{2,1,0:T(8,128)S(1)} %bitcast.55), channel_id=1, replica_groups=mesh['gx'=16,'gy'=32] {'gy'}, dimensions={0} | all-to-all | bytes 524288 | tf_op jit(solution)/shard_map/all_to_all | solution.py:231
  29.6 0.0 copy-start.1
  29.7 0.7 broadcast_in_dim.14
  30.4 5.6 %all-to-all-start.1 = ((f32[32,8,256]{2,1,0:T(8,128)}), f32[32,8,256]{2,1,0:T(8,128)S(1)}, u32[]{:S(2)}, u32[]{:S(2)}) async-start(f32[32,8,256]{2,1,0:T(8,128)} %broadcast_in_dim.14), calls=%async_computation.1 | async-start | bytes 524288 | tf_op jit(solution)/shard_map/all_to_all | solution.py:231
  36.0 0.0 copy-done.3
  36.0 7.7 %collective-permute-start.2 = (f32[1,8,16,256]{3,2,1,0:T(8,128)S(1)}, f32[1,8,16,256]{3,2,1,0:T(8,128)S(1)}, u32[]{:S(2)}, u32[]{:S(2)}) collective-permute-start(f32[1,8,16,256]{3,2,1,0:T(8,128)S(1)} %bitcast.59), channel_id=1, source_target_pairs={{0,256},{32,288},{64,320},{96,352},{128,384},{160,416},{192,448},{... | collective-permute-start | bytes 393224 | tf_op jit(solution)/shard_map/ppermute | solution.py:251
  43.8 4.6 %collective-permute-done.2 = f32[1,8,16,256]{3,2,1,0:T(8,128)S(1)} collective-permute-done((f32[1,8,16,256]{3,2,1,0:T(8,128)S(1)}, f32[1,8,16,256]{3,2,1,0:T(8,128)S(1)}, u32[]{:S(2)}, u32[]{:S(2)}) %collective-permute-start.2) | collective-permute-done | bytes 131104 | tf_op jit(solution)/shard_map/ppermute | solution.py:251
  48.4 4.7 %collective-permute-start.3 = (f32[2,8,16,256]{3,2,1,0:T(8,128)S(1)}, f32[2,8,16,256]{3,2,1,0:T(8,128)S(1)}, u32[]{:S(2)}, u32[]{:S(2)}) collective-permute-start(f32[2,8,16,256]{3,2,1,0:T(8,128)S(1)} %pad_maximum_fusion.2), channel_id=1, source_target_pairs={{0,128},{32,416},{64,192},{96,480},{128,256},{160,32},{192,320},{2... | collective-permute-start | bytes 786440 | tf_op jit(solution)/shard_map/ppermute | solution.py:251
  53.0 0.0 all-to-all-done.1
  53.1 0.0 copy-done.1
  53.1 1.8 %fusion = f32[256,128,8]{0,1,2:T(8,128)S(1)} fusion(f32[256,128,8]{1,2,0:T(8,128)S(1)} %copy-done.1, f32[32,8,256]{2,1,0:T(8,128)S(1)} %all-to-all-done.1), kind=kOutput, calls=%fused_computation.3 | convolution fusion | flops 805306368 | bytes 2359296 | tf_op jit(solution)/shard_map/ijk,ir->kjr/dot_general | solution.py:262
  54.9 0.1 copy.28
  55.1 1.9 %collective-permute-start = (f32[2,4,64,256]{3,2,1,0:T(8,128)S(1)}, f32[2,4,64,256]{3,2,1,0:T(8,128)S(1)}, u32[]{:S(2)}, u32[]{:S(2)}) collective-permute-start(f32[2,4,64,256]{3,2,1,0:T(8,128)S(1)} %dynamic-slice_bitcast_fusion), channel_id=1, source_target_pairs={{0,32},{32,0},{64,96},{96,64},{128,160},{160,128},{192,224},{224,1... | collective-permute-start | bytes 1572872 | tf_op jit(solution)/shard_map/ppermute | solution.py:267
  57.0 0.6 convolution_bitcast_fusion
  57.6 0.7 broadcast_in_dim.16
  58.3 5.4 %all-to-all-start.2 = ((f32[16,8,256]{2,1,0:T(8,128)}), f32[16,8,256]{2,1,0:T(8,128)S(1)}, u32[]{:S(2)}, u32[]{:S(2)}) async-start(f32[16,8,256]{2,1,0:T(8,128)} %broadcast_in_dim.16), calls=%async_computation.2 | async-start | bytes 262144 | tf_op jit(solution)/shard_map/all_to_all | solution.py:231
  63.7 0.0 collective-permute-done.3
  63.7 0.8 pad_maximum_fusion.1
  64.6 3.8 %collective-permute-start.4 = (f32[4,8,16,256]{3,2,1,0:T(8,128)}, f32[4,8,16,256]{3,2,1,0:T(8,128)}, u32[]{:S(2)}, u32[]{:S(2)}) collective-permute-start(f32[4,8,16,256]{3,2,1,0:T(8,128)} %pad_maximum_fusion.1), channel_id=1, source_target_pairs={{0,64},{32,480},{64,128},{96,32},{128,192},{160,96},{192,256},{224... | collective-permute-start | bytes 1572872 | tf_op jit(solution)/shard_map/ppermute | solution.py:251
  68.5 3.9 %all-to-all-done.2 = f32[16,8,256]{2,1,0:T(8,128)S(1)} async-done(((f32[16,8,256]{2,1,0:T(8,128)}), f32[16,8,256]{2,1,0:T(8,128)S(1)}, u32[]{:S(2)}, u32[]{:S(2)}) %all-to-all-start.2) | async-done | bytes 131104 | tf_op jit(solution)/shard_map/all_to_all | solution.py:231
  72.4 0.7 broadcast_in_dim.17
  73.1 9.8 %all-to-all-start.3 = ((f32[32,8,256]{2,1,0:T(8,128)}), f32[32,8,256]{2,1,0:T(8,128)S(1)}, u32[]{:S(2)}, u32[]{:S(2)}) async-start(f32[32,8,256]{2,1,0:T(8,128)} %broadcast_in_dim.17), calls=%async_computation.3 | async-start | bytes 524288 | tf_op jit(solution)/shard_map/all_to_all | solution.py:231
  82.9 0.0 collective-permute-done
  82.9 0.1 bitcast_add_fusion
  83.0 0.7 dynamic-slice_bitcast_fusion.1
  83.7 2.6 %collective-permute-start.1 = (f32[4,64,256]{2,1,0:T(8,128)}, f32[4,64,256]{2,1,0:T(8,128)}, u32[]{:S(2)}, u32[]{:S(2)}) collective-permute-start(f32[4,64,256]{2,1,0:T(8,128)} %dynamic-slice_bitcast_fusion.1), channel_id=1, source_target_pairs={{0,64},{32,96},{64,0},{96,32},{128,192},{160,224},{192,128},{224,1... | collective-permute-start | bytes 786440 | tf_op jit(solution)/shard_map/ppermute | solution.py:267
  86.3 0.0 collective-permute-done.4
  86.3 1.1 pad_maximum_fusion.s_ref
  87.4 1.9 %collective-permute-start.5 = (f32[8,8,16,256]{3,2,1,0:T(8,128)S(1)}, f32[8,8,16,256]{3,2,1,0:T(8,128)S(1)}, u32[]{:S(2)}, u32[]{:S(2)}) collective-permute-start(f32[8,8,16,256]{3,2,1,0:T(8,128)S(1)} %pad_maximum_fusion.s_ref), channel_id=1, source_target_pairs={{0,32},{32,0},{64,96},{96,64},{128,160},{160,128},{192,224},{224,1... | collective-permute-start | bytes 3145736 | tf_op jit(solution)/shard_map/ppermute | solution.py:252
  89.4 4.8 %collective-permute-done.1 = f32[4,64,256]{2,1,0:T(8,128)} collective-permute-done((f32[4,64,256]{2,1,0:T(8,128)}, f32[4,64,256]{2,1,0:T(8,128)}, u32[]{:S(2)}, u32[]{:S(2)}) %collective-permute-start.1) | collective-permute-done | bytes 262176 | tf_op jit(solution)/shard_map/ppermute | solution.py:267
  94.2 1.7 bitcast_add_fusion.1
  95.9 0.0 all-to-all-done.3
  95.9 3.6 %all-to-all-start.4 = ((f32[4,64,256]{2,1,0:T(8,128)}), f32[4,64,256]{2,1,0:T(8,128)S(1)}, u32[]{:S(2)}, u32[]{:S(2)}) async-start(f32[4,64,256]{2,1,0:T(8,128)} %bitcast_add_fusion.1), calls=%async_computation.4 | async-start | bytes 524288 | tf_op jit(solution)/shard_map/all_to_all | solution.py:231
  99.5 9.1 %first_factor.1 = (f32[256,256]{1,0:T(8,128)S(1)}, f32[256,256]{1,0:T(8,128)S(1)}) custom-call(s32[1]{0:T(128)} %bitcast.3.i_ref, f32[256,256]{1,0:T(8,128)S(1)} %bitcast.54), custom_call_target="tpu_custom_call" | custom-call | flops 6000000000 | bytes 786432 | tf_op jit(solution)/shard_map/first_factor/pallas_call | solution.py:193
  108.6 0.0 collective-permute-done.5.t_ref
  108.6 0.8 all-to-all-done.4.m_ref
  109.4 1.9 %second_sketch.1 = f32[16,8,384]{2,1,0:T(8,128)S(1)} custom-call(f32[4,64,256]{2,1,0:T(8,128)S(1)} %all-to-all-done.4.m_ref, f32[256,256]{1,0:T(8,128)S(1)} %get-tuple-element.7.x_ref, f32[256,256]{1,0:T(8,128)S(1)} %get-tuple-element.8.p_ref, f32[8,8,16,256]{3,2,1,0:T(8,128)S(1)} %pad_maximum_fusion.s_ref, f32[8,8,16,256]{3,2,1,0:T(8,128)S(1)} %collective-permute-done.5.t_ref), custom_call_target="tpu_custom_call" | custom-call | flops 200000000 | bytes 4000000 | tf_op jit(solution)/shard_map/second_sketch/pallas_call | solution.py:219
  111.3 15.9 %all_to_all.41 = f32[16,8,384]{2,1,0:T(8,128)S(1)} all-to-all(f32[16,8,384]{2,1,0:T(8,128)S(1)} %second_sketch.1), channel_id=1, replica_groups=mesh['gx'=16,'gy'=32] {'gx'}, dimensions={0} | all-to-all | bytes 393216 | tf_op jit(solution)/shard_map/all_to_all | solution.py:231
  127.3 0.1 copy.23
  127.4 0.5 fusion.5
  127.8 24.5 %all_to_all.42 = f32[32,8,384]{2,1,0:T(8,128)S(1)} all-to-all(f32[32,8,384]{2,1,0:T(8,128)S(1)} %fusion.5), channel_id=1, replica_groups=mesh['gx'=16,'gy'=32] {'gy'}, dimensions={0} | all-to-all | bytes 786432 | tf_op jit(solution)/shard_map/all_to_all | solution.py:231
  152.4 0.8 broadcast_in_dim.39
  153.2 5.6 %all-to-all-start.7 = ((f32[32,8,384]{2,1,0:T(8,128)}), f32[32,8,384]{2,1,0:T(8,128)S(1)}, u32[]{:S(2)}, u32[]{:S(2)}) async-start(f32[32,8,384]{2,1,0:T(8,128)} %broadcast_in_dim.39), calls=%async_computation.7 | async-start | bytes 786432 | tf_op jit(solution)/shard_map/all_to_all | solution.py:231
  158.7 1.1 fusion.3
  159.8 12.5 %all-to-all-done.7 = f32[32,8,384]{2,1,0:T(8,128)S(1)} async-done(((f32[32,8,384]{2,1,0:T(8,128)}), f32[32,8,384]{2,1,0:T(8,128)S(1)}, u32[]{:S(2)}, u32[]{:S(2)}) %all-to-all-start.7) | async-done | bytes 393248 | tf_op jit(solution)/shard_map/all_to_all | solution.py:231
  172.3 10.2 %second_factor.1 = (f32[128,256]{1,0:T(8,128)}, f32[8,8,16]{2,1,0:T(8,128)}) custom-call(s32[1]{0:T(128)} %bitcast.6.i_ref, f32[256,384]{1,0:T(8,128)S(1)} %bitcast.53, f32[128,384]{1,0:T(8,128)S(1)} %bitcast.51), custom_call_target="tpu_custom_call" | custom-call | flops 6000000000 | bytes 786432 | tf_op jit(solution)/shard_map/second_factor/pallas_call | solution.py:206
  (8 shorter events, 0.2 us)
Async XLA Ops:
  0.6 1.2 copy-start
  1.9 1.2 copy-start.2
  5.0 31.0 %copy-start.3 = (f32[16,8,256]{2,1,0:T(8,128)S(1)}, f32[16,8,256]{2,1,0:T(8,128)}, u32[]{:S(2)}) copy-start(f32[16,8,256]{2,1,0:T(8,128)} %param.5) | copy-start | bytes 393220
  29.6 23.4 %copy-start.1 = (f32[256,128,8]{1,2,0:T(8,128)S(1)}, f32[256,128,8]{1,2,0:T(8,128)}, u32[]{:S(2)}) copy-start(f32[256,128,8]{1,2,0:T(8,128)} %param.3) | copy-start | bytes 3145732
  30.4 22.7 %all-to-all-start.1 = ((f32[32,8,256]{2,1,0:T(8,128)}), f32[32,8,256]{2,1,0:T(8,128)S(1)}, u32[]{:S(2)}, u32[]{:S(2)}) async-start(f32[32,8,256]{2,1,0:T(8,128)} %broadcast_in_dim.14), calls=%async_computation.1 | async-start | bytes 524288 | tf_op jit(solution)/shard_map/all_to_all | solution.py:231
  36.0 12.3 %collective-permute-start.2 = (f32[1,8,16,256]{3,2,1,0:T(8,128)S(1)}, f32[1,8,16,256]{3,2,1,0:T(8,128)S(1)}, u32[]{:S(2)}, u32[]{:S(2)}) collective-permute-start(f32[1,8,16,256]{3,2,1,0:T(8,128)S(1)} %bitcast.59), channel_id=1, source_target_pairs={{0,256},{32,288},{64,320},{96,352},{128,384},{160,416},{192,448},{... | collective-permute-start | bytes 393224 | tf_op jit(solution)/shard_map/ppermute | solution.py:251
  48.4 15.4 %collective-permute-start.3 = (f32[2,8,16,256]{3,2,1,0:T(8,128)S(1)}, f32[2,8,16,256]{3,2,1,0:T(8,128)S(1)}, u32[]{:S(2)}, u32[]{:S(2)}) collective-permute-start(f32[2,8,16,256]{3,2,1,0:T(8,128)S(1)} %pad_maximum_fusion.2), channel_id=1, source_target_pairs={{0,128},{32,416},{64,192},{96,480},{128,256},{160,32},{192,320},{2... | collective-permute-start | bytes 786440 | tf_op jit(solution)/shard_map/ppermute | solution.py:251
  55.1 27.8 %collective-permute-start = (f32[2,4,64,256]{3,2,1,0:T(8,128)S(1)}, f32[2,4,64,256]{3,2,1,0:T(8,128)S(1)}, u32[]{:S(2)}, u32[]{:S(2)}) collective-permute-start(f32[2,4,64,256]{3,2,1,0:T(8,128)S(1)} %dynamic-slice_bitcast_fusion), channel_id=1, source_target_pairs={{0,32},{32,0},{64,96},{96,64},{128,160},{160,128},{192,224},{224,1... | collective-permute-start | bytes 1572872 | tf_op jit(solution)/shard_map/ppermute | solution.py:267
  58.3 14.1 %all-to-all-start.2 = ((f32[16,8,256]{2,1,0:T(8,128)}), f32[16,8,256]{2,1,0:T(8,128)S(1)}, u32[]{:S(2)}, u32[]{:S(2)}) async-start(f32[16,8,256]{2,1,0:T(8,128)} %broadcast_in_dim.16), calls=%async_computation.2 | async-start | bytes 262144 | tf_op jit(solution)/shard_map/all_to_all | solution.py:231
  64.6 21.7 %collective-permute-start.4 = (f32[4,8,16,256]{3,2,1,0:T(8,128)}, f32[4,8,16,256]{3,2,1,0:T(8,128)}, u32[]{:S(2)}, u32[]{:S(2)}) collective-permute-start(f32[4,8,16,256]{3,2,1,0:T(8,128)} %pad_maximum_fusion.1), channel_id=1, source_target_pairs={{0,64},{32,480},{64,128},{96,32},{128,192},{160,96},{192,256},{224... | collective-permute-start | bytes 1572872 | tf_op jit(solution)/shard_map/ppermute | solution.py:251
  73.1 22.8 %all-to-all-start.3 = ((f32[32,8,256]{2,1,0:T(8,128)}), f32[32,8,256]{2,1,0:T(8,128)S(1)}, u32[]{:S(2)}, u32[]{:S(2)}) async-start(f32[32,8,256]{2,1,0:T(8,128)} %broadcast_in_dim.17), calls=%async_computation.3 | async-start | bytes 524288 | tf_op jit(solution)/shard_map/all_to_all | solution.py:231
  83.7 10.5 %collective-permute-start.1 = (f32[4,64,256]{2,1,0:T(8,128)}, f32[4,64,256]{2,1,0:T(8,128)}, u32[]{:S(2)}, u32[]{:S(2)}) collective-permute-start(f32[4,64,256]{2,1,0:T(8,128)} %dynamic-slice_bitcast_fusion.1), channel_id=1, source_target_pairs={{0,64},{32,96},{64,0},{96,32},{128,192},{160,224},{192,128},{224,1... | collective-permute-start | bytes 786440 | tf_op jit(solution)/shard_map/ppermute | solution.py:267
  87.4 21.1 %collective-permute-start.5 = (f32[8,8,16,256]{3,2,1,0:T(8,128)S(1)}, f32[8,8,16,256]{3,2,1,0:T(8,128)S(1)}, u32[]{:S(2)}, u32[]{:S(2)}) collective-permute-start(f32[8,8,16,256]{3,2,1,0:T(8,128)S(1)} %pad_maximum_fusion.s_ref), channel_id=1, source_target_pairs={{0,32},{32,0},{64,96},{96,64},{128,160},{160,128},{192,224},{224,1... | collective-permute-start | bytes 3145736 | tf_op jit(solution)/shard_map/ppermute | solution.py:252
  95.9 13.5 %all-to-all-start.4 = ((f32[4,64,256]{2,1,0:T(8,128)}), f32[4,64,256]{2,1,0:T(8,128)S(1)}, u32[]{:S(2)}, u32[]{:S(2)}) async-start(f32[4,64,256]{2,1,0:T(8,128)} %bitcast_add_fusion.1), calls=%async_computation.4 | async-start | bytes 524288 | tf_op jit(solution)/shard_map/all_to_all | solution.py:231
  153.2 19.1 %all-to-all-start.7 = ((f32[32,8,384]{2,1,0:T(8,128)}), f32[32,8,384]{2,1,0:T(8,128)S(1)}, u32[]{:S(2)}, u32[]{:S(2)}) async-start(f32[32,8,384]{2,1,0:T(8,128)} %broadcast_in_dim.39), calls=%async_computation.7 | async-start | bytes 786432 | tf_op jit(solution)/shard_map/all_to_all | solution.py:231

commit v5 on v4

--- a/solution.py
+++ b/solution.py
@@ -261,10 +261,16 @@
 
     mixed_part = jnp.einsum("ijk,ir->kjr", tensor, first, precision=HI)
     mixed_part = mixed_part.reshape(8, 4, 2, 2, 8, 256).transpose(3, 2, 1, 0, 4, 5).reshape(2, 2, 4, 64, 256)
-    for bit, here in ((1, row % 2), (2, (row // 2) % 2)):
-        keep = lax.dynamic_index_in_dim(mixed_part, here, 0, keepdims=False)
-        give = lax.dynamic_index_in_dim(mixed_part, 1 - here, 0, keepdims=False)
-        mixed_part = keep + lax.ppermute(give, "gx", [(i, i ^ bit) for i in range(gx)])
+    core_bit, chip_bit = row % 2, (row // 2) % 2
+
+    def pick(block, bit):
+        return lax.dynamic_index_in_dim(block, bit, 0, keepdims=False)
+
+    mine = pick(mixed_part, core_bit)
+    theirs = lax.ppermute(pick(mixed_part, 1 - core_bit), "gx", [(i, i ^ 1) for i in range(gx)])
+    give = pick(mine, 1 - chip_bit) + pick(theirs, 1 - chip_bit)
+    other = lax.ppermute(give, "gx", [(i, i ^ 2) for i in range(gx)])
+    mixed_part = (pick(mine, chip_bit) + pick(theirs, chip_bit)) + other
     mixed = swap(mixed_part, "gx", [list(range(i, gx, 4)) for i in range(4)])
 
     inv_one, placed = first_factor(row.astype(jnp.int32)[None], gram)

time: 183 us -> 186 us (1.016)
  blocking collectives: 65 us -> 40.4 us
  starting transfers between devices: 52.6 us -> 67.6 us
  waiting for transfers between devices: 26.6 us -> 37.7 us
    all_to_all x3 -> x2, blocking collectives: 65 us -> 40.4 us  [swap(): lax.all_to_all(pieces, axis, 0, 0, axis_index_groups=groups, tiled=True)]
    all_to_all x5 -> x6, starting transfers between devices: 29.9 us -> 45.2 us  [swap(): lax.all_to_all(pieces, axis, 0, 0, axis_index_groups=groups, tiled=True)]
    all_to_all x5 -> x6, waiting for transfers between devices: 17.2 us -> 25.3 us  [swap(): lax.all_to_all(pieces, axis, 0, 0, axis_index_groups=groups, tiled=True)]
    ppermute x3, waiting for transfers between devices: 4.57 us -> 7.56 us  [local(): near = jnp.concatenate([near, lax.ppermute(near, 'gx', turn(d))], axis=0)]
  transfers between devices with their start and end apart: 11 -> 12, of which waited for: 5 -> 6; matrix products, arithmetic and copies ran while one was open for 5% -> 6% of each run, Pallas kernels for 5% -> 5%
where the time goes in v5:
time: 186 us; the launch traced here: 185 us
  starting transfers between devices  67.6 us (36%)
  blocking collectives  40.4 us (22%)
  waiting for transfers between devices  37.7 us (20%)
  Pallas kernels  23.8 us (13%)
  local copies, waits for them, and re-layouts  6.47 us (3%)
  matrix products  4 us (2%)
  other arithmetic  3.81 us (2%)
    all_to_all x6, starting transfers between devices, swap(): lax.all_to_all(pieces, axis, 0, 0, axis_index_groups=groups, tiled=True)  45.2 us
    all_to_all x2, blocking collectives, swap(): lax.all_to_all(pieces, axis, 0, 0, axis_index_groups=groups, tiled=True)  40.4 us
    all_to_all x6, waiting for transfers between devices, swap(): lax.all_to_all(pieces, axis, 0, 0, axis_index_groups=groups, tiled=True)  25.3 us
    ppermute x3, starting transfers between devices, local(): near = jnp.concatenate([near, lax.ppermute(near, 'gx', turn(d))], axis=0)  16 us
    pallas_call x1, Pallas kernels, second_factor(): pl.pallas_call(second_factor_kernel, out_shape=(jax.ShapeDtypeStruct((128...  10.2 us
    pallas_call x1, Pallas kernels, first_factor(): pl.pallas_call(first_factor_kernel, out_shape=(SQUARE, SQUARE), in_specs=...  9.09 us
    ppermute x3, waiting for transfers between devices, local(): near = jnp.concatenate([near, lax.ppermute(near, 'gx', turn(d))], axis=0)  7.56 us
    ppermute x1, waiting for transfers between devices, local(): other = lax.ppermute(give, 'gx', [(i, i ^ 2) for i in range(gx)])  4.82 us
  transfers between devices with their start and end apart: 12, of which 6 were waited for; matrix products, arithmetic and copies ran while one was open for 6% of the time, Pallas kernels for 5%

profile of v5, /device:TPU:2, one launch (start us, length us, event | category | flops | bytes accessed | tf_op | source)
XLA Modules:
  0.0 184.8 jit_solution(2283652477634201160)
XLA Ops:
  0.6 0.0 copy-start
  0.6 1.2 copy-done
  1.9 0.0 copy-start.2
  1.9 1.2 copy-done.2
  3.1 2.6 %first_dot.1 = f32[256,256]{1,0:T(8,128)} custom-call(f32[256,8,128]{2,1,0:T(8,128)S(1)} %bitcast.56, f32[128,8,256]{2,1,0:T(8,128)S(1)} %copy-done.2), custom_call_target="tpu_custom_call" | custom-call | flops 800000000 | bytes 2500000 | tf_op jit(solution)/shard_map/first_dot/pallas_call | solution.py:181
  5.7 0.0 copy-start.8
  5.7 13.6 %all-to-all-start = ((f32[32,8,256]{2,1,0:T(8,128)}), f32[32,8,256]{2,1,0:T(8,128)S(1)}, u32[]{:S(2)}, u32[]{:S(2)}) async-start(f32[32,8,256]{2,1,0:T(8,128)} %bitcast.1), calls=%async_computation | async-start | bytes 524288 | tf_op jit(solution)/shard_map/all_to_all | solution.py:231
  19.3 0.0 copy-done.8
  19.4 7.7 %collective-permute-start.2 = (f32[1,8,16,256]{3,2,1,0:T(8,128)S(1)}, f32[1,8,16,256]{3,2,1,0:T(8,128)S(1)}, u32[]{:S(2)}, u32[]{:S(2)}) collective-permute-start(f32[1,8,16,256]{3,2,1,0:T(8,128)S(1)} %bitcast.63), channel_id=1, source_target_pairs={{0,256},{32,288},{64,320},{96,352},{128,384},{160,416},{192,448},{... | collective-permute-start | bytes 393224 | tf_op jit(solution)/shard_map/ppermute | solution.py:251
  27.1 3.4 %all-to-all-done = f32[32,8,256]{2,1,0:T(8,128)S(1)} async-done(((f32[32,8,256]{2,1,0:T(8,128)}), f32[32,8,256]{2,1,0:T(8,128)S(1)}, u32[]{:S(2)}, u32[]{:S(2)}) %all-to-all-start) | async-done | bytes 262176 | tf_op jit(solution)/shard_map/all_to_all | solution.py:231
  30.6 0.7 broadcast_in_dim.14
  31.3 0.0 copy-start.1
  31.3 6.5 %all-to-all-start.1 = ((f32[32,8,256]{2,1,0:T(8,128)}), f32[32,8,256]{2,1,0:T(8,128)S(1)}, u32[]{:S(2)}, u32[]{:S(2)}) async-start(f32[32,8,256]{2,1,0:T(8,128)} %broadcast_in_dim.14), calls=%async_computation.1 | async-start | bytes 524288 | tf_op jit(solution)/shard_map/all_to_all | solution.py:231
  37.8 0.0 collective-permute-done.2
  37.8 0.0 copy-start.5
  37.8 3.7 %collective-permute-start.3 = (f32[2,8,16,256]{3,2,1,0:T(8,128)S(1)}, f32[2,8,16,256]{3,2,1,0:T(8,128)S(1)}, u32[]{:S(2)}, u32[]{:S(2)}) collective-permute-start(f32[2,8,16,256]{3,2,1,0:T(8,128)S(1)} %pad_maximum_fusion.2), channel_id=1, source_target_pairs={{0,128},{32,416},{64,192},{96,480},{128,256},{160,32},{192,320},{2... | collective-permute-start | bytes 786440 | tf_op jit(solution)/shard_map/ppermute | solution.py:251
  41.6 7.6 %collective-permute-done.3 = f32[2,8,16,256]{3,2,1,0:T(8,128)S(1)} collective-permute-done((f32[2,8,16,256]{3,2,1,0:T(8,128)S(1)}, f32[2,8,16,256]{3,2,1,0:T(8,128)S(1)}, u32[]{:S(2)}, u32[]{:S(2)}) %collective-permute-start.3) | collective-permute-done | bytes 262176 | tf_op jit(solution)/shard_map/ppermute | solution.py:251
  49.1 0.0 copy-done.5
  49.2 4.6 %collective-permute-start.4 = (f32[4,8,16,256]{3,2,1,0:T(8,128)S(1)}, f32[4,8,16,256]{3,2,1,0:T(8,128)}, u32[]{:S(2)}, u32[]{:S(2)}) collective-permute-start(f32[4,8,16,256]{3,2,1,0:T(8,128)S(1)} %pad_maximum_fusion.1), channel_id=1, source_target_pairs={{0,64},{32,480},{64,128},{96,32},{128,192},{160,96},{192,256},{224... | collective-permute-start | bytes 1572872 | tf_op jit(solution)/shard_map/ppermute | solution.py:251
  53.8 0.0 all-to-all-done.1
  53.8 0.0 copy-done.1
  53.8 0.0 copy-start.3
  53.8 1.8 fusion
  55.6 0.1 copy.29
  55.7 0.9 dynamic-slice_bitcast_fusion
  56.6 1.9 %collective-permute-start = (f32[2,4,64,256]{3,2,1,0:T(8,128)}, f32[2,4,64,256]{3,2,1,0:T(8,128)S(1)}, u32[]{:S(2)}, u32[]{:S(2)}) collective-permute-start(f32[2,4,64,256]{3,2,1,0:T(8,128)} %dynamic-slice_bitcast_fusion), channel_id=1, source_target_pairs={{0,32},{32,0},{64,96},{96,64},{128,160},{160,128},{192,224},{224,1... | collective-permute-start | bytes 1572872 | tf_op jit(solution)/shard_map/ppermute | solution.py:270
  58.5 0.0 copy-done.3
  58.5 0.6 convolution_bitcast_fusion
  59.1 0.7 broadcast_in_dim.16
  59.8 6.1 %all-to-all-start.2 = ((f32[16,8,256]{2,1,0:T(8,128)}), f32[16,8,256]{2,1,0:T(8,128)S(1)}, u32[]{:S(2)}, u32[]{:S(2)}) async-start(f32[16,8,256]{2,1,0:T(8,128)} %broadcast_in_dim.16), calls=%async_computation.2 | async-start | bytes 262144 | tf_op jit(solution)/shard_map/all_to_all | solution.py:231
  65.9 8.6 %all-to-all-done.2 = f32[16,8,256]{2,1,0:T(8,128)S(1)} async-done(((f32[16,8,256]{2,1,0:T(8,128)}), f32[16,8,256]{2,1,0:T(8,128)S(1)}, u32[]{:S(2)}, u32[]{:S(2)}) %all-to-all-start.2) | async-done | bytes 131104 | tf_op jit(solution)/shard_map/all_to_all | solution.py:231
  74.5 0.7 broadcast_in_dim.17
  75.3 9.8 %all-to-all-start.3 = ((f32[32,8,256]{2,1,0:T(8,128)}), f32[32,8,256]{2,1,0:T(8,128)S(1)}, u32[]{:S(2)}, u32[]{:S(2)}) async-start(f32[32,8,256]{2,1,0:T(8,128)} %broadcast_in_dim.17), calls=%async_computation.3 | async-start | bytes 524288 | tf_op jit(solution)/shard_map/all_to_all | solution.py:231
  85.0 0.0 copy-start.6
  85.0 0.0 collective-permute-done
  85.1 0.0 copy-start.7
  85.1 0.7 bitcast_add_fusion
  85.8 2.6 %collective-permute-start.1 = (f32[4,64,256]{2,1,0:T(8,128)}, f32[4,64,256]{2,1,0:T(8,128)}, u32[]{:S(2)}, u32[]{:S(2)}) collective-permute-start(f32[4,64,256]{2,1,0:T(8,128)} %bitcast_add_fusion), channel_id=1, source_target_pairs={{0,64},{32,96},{64,0},{96,32},{128,192},{160,224},{192,128},{224,1... | collective-permute-start | bytes 786440 | tf_op jit(solution)/shard_map/ppermute | solution.py:272
  88.4 0.0 copy-done.7
  88.4 0.0 collective-permute-done.4
  88.4 0.0 copy-done.6
  88.4 1.1 pad_maximum_fusion.s_ref
  89.5 1.9 %collective-permute-start.5 = (f32[8,8,16,256]{3,2,1,0:T(8,128)S(1)}, f32[8,8,16,256]{3,2,1,0:T(8,128)S(1)}, u32[]{:S(2)}, u32[]{:S(2)}) collective-permute-start(f32[8,8,16,256]{3,2,1,0:T(8,128)S(1)} %pad_maximum_fusion.s_ref), channel_id=1, source_target_pairs={{0,32},{32,0},{64,96},{96,64},{128,160},{160,128},{192,224},{224,1... | collective-permute-start | bytes 3145736 | tf_op jit(solution)/shard_map/ppermute | solution.py:252
  91.5 4.8 %collective-permute-done.1 = f32[4,64,256]{2,1,0:T(8,128)} collective-permute-done((f32[4,64,256]{2,1,0:T(8,128)}, f32[4,64,256]{2,1,0:T(8,128)}, u32[]{:S(2)}, u32[]{:S(2)}) %collective-permute-start.1) | collective-permute-done | bytes 262176 | tf_op jit(solution)/shard_map/ppermute | solution.py:272
  96.3 1.8 fusion.3
  98.1 0.0 all-to-all-done.3
  98.1 3.6 %all-to-all-start.4 = ((f32[4,64,256]{2,1,0:T(8,128)}), f32[4,64,256]{2,1,0:T(8,128)S(1)}, u32[]{:S(2)}, u32[]{:S(2)}) async-start(f32[4,64,256]{2,1,0:T(8,128)} %fusion.3), calls=%async_computation.4 | async-start | bytes 524288 | tf_op jit(solution)/shard_map/all_to_all | solution.py:231
  101.7 9.1 %first_factor.1 = (f32[256,256]{1,0:T(8,128)S(1)}, f32[256,256]{1,0:T(8,128)S(1)}) custom-call(s32[1]{0:T(128)} %bitcast.3.i_ref, f32[256,256]{1,0:T(8,128)S(1)} %bitcast.58), custom_call_target="tpu_custom_call" | custom-call | flops 6000000000 | bytes 786432 | tf_op jit(solution)/shard_map/first_factor/pallas_call | solution.py:193
  110.8 0.0 collective-permute-done.5.t_ref
  110.8 0.8 all-to-all-done.4.m_ref
  111.6 1.9 %second_sketch.1 = f32[16,8,384]{2,1,0:T(8,128)S(1)} custom-call(f32[4,64,256]{2,1,0:T(8,128)S(1)} %all-to-all-done.4.m_ref, f32[256,256]{1,0:T(8,128)S(1)} %get-tuple-element.7.x_ref, f32[256,256]{1,0:T(8,128)S(1)} %get-tuple-element.8.p_ref, f32[8,8,16,256]{3,2,1,0:T(8,128)S(1)} %pad_maximum_fusion.s_ref, f32[8,8,16,256]{3,2,1,0:T(8,128)S(1)} %collective-permute-done.5.t_ref), custom_call_target="tpu_custom_call" | custom-call | flops 200000000 | bytes 4000000 | tf_op jit(solution)/shard_map/second_sketch/pallas_call | solution.py:219
  113.5 16.0 %all_to_all.40 = f32[16,8,384]{2,1,0:T(8,128)S(1)} all-to-all(f32[16,8,384]{2,1,0:T(8,128)S(1)} %second_sketch.1), channel_id=1, replica_groups=mesh['gx'=16,'gy'=32] {'gx'}, dimensions={0} | all-to-all | bytes 393216 | tf_op jit(solution)/shard_map/all_to_all | solution.py:231
  129.5 0.1 copy.24
  129.6 0.5 fusion.6
  130.0 24.5 %all_to_all.41 = f32[32,8,384]{2,1,0:T(8,128)S(1)} all-to-all(f32[32,8,384]{2,1,0:T(8,128)S(1)} %fusion.6), channel_id=1, replica_groups=mesh['gx'=16,'gy'=32] {'gy'}, dimensions={0} | all-to-all | bytes 786432 | tf_op jit(solution)/shard_map/all_to_all | solution.py:231
  154.6 0.8 broadcast_in_dim.39
  155.4 0.0 copy-start.4
  155.4 5.7 %all-to-all-start.7 = ((f32[32,8,384]{2,1,0:T(8,128)}), f32[32,8,384]{2,1,0:T(8,128)S(1)}, u32[]{:S(2)}, u32[]{:S(2)}) async-start(f32[32,8,384]{2,1,0:T(8,128)} %broadcast_in_dim.39), calls=%async_computation.7 | async-start | bytes 786432 | tf_op jit(solution)/shard_map/all_to_all | solution.py:231
  161.1 0.0 copy-done.4
  161.1 1.1 fusion.4
  162.2 12.4 %all-to-all-done.7 = f32[32,8,384]{2,1,0:T(8,128)S(1)} async-done(((f32[32,8,384]{2,1,0:T(8,128)}), f32[32,8,384]{2,1,0:T(8,128)S(1)}, u32[]{:S(2)}, u32[]{:S(2)}) %all-to-all-start.7) | async-done | bytes 393248 | tf_op jit(solution)/shard_map/all_to_all | solution.py:231
  174.6 10.2 %second_factor.1 = (f32[128,256]{1,0:T(8,128)}, f32[8,8,16]{2,1,0:T(8,128)}) custom-call(s32[1]{0:T(128)} %bitcast.6.i_ref, f32[256,384]{1,0:T(8,128)S(1)} %bitcast.57, f32[128,384]{1,0:T(8,128)S(1)} %bitcast.55), custom_call_target="tpu_custom_call" | custom-call | flops 6000000000 | bytes 786432 | tf_op jit(solution)/shard_map/second_factor/pallas_call | solution.py:206
  (8 shorter events, 0.2 us)
Async XLA Ops:
  0.6 1.2 copy-start
  1.9 1.2 copy-start.2
  5.7 13.6 %copy-start.8 = (f32[16,8,256]{2,1,0:T(8,128)S(1)}, f32[16,8,256]{2,1,0:T(8,128)}, u32[]{:S(2)}) copy-start(f32[16,8,256]{2,1,0:T(8,128)} %param.5) | copy-start | bytes 393220
  5.7 24.8 %all-to-all-start = ((f32[32,8,256]{2,1,0:T(8,128)}), f32[32,8,256]{2,1,0:T(8,128)S(1)}, u32[]{:S(2)}, u32[]{:S(2)}) async-start(f32[32,8,256]{2,1,0:T(8,128)} %bitcast.1), calls=%async_computation | async-start | bytes 524288 | tf_op jit(solution)/shard_map/all_to_all | solution.py:231
  19.4 18.4 %collective-permute-start.2 = (f32[1,8,16,256]{3,2,1,0:T(8,128)S(1)}, f32[1,8,16,256]{3,2,1,0:T(8,128)S(1)}, u32[]{:S(2)}, u32[]{:S(2)}) collective-permute-start(f32[1,8,16,256]{3,2,1,0:T(8,128)S(1)} %bitcast.63), channel_id=1, source_target_pairs={{0,256},{32,288},{64,320},{96,352},{128,384},{160,416},{192,448},{... | collective-permute-start | bytes 393224 | tf_op jit(solution)/shard_map/ppermute | solution.py:251
  31.3 22.5 %copy-start.1 = (f32[256,128,8]{1,2,0:T(8,128)S(1)}, f32[256,128,8]{1,2,0:T(8,128)}, u32[]{:S(2)}) copy-start(f32[256,128,8]{1,2,0:T(8,128)} %param.3) | copy-start | bytes 3145732
  31.3 22.5 %all-to-all-start.1 = ((f32[32,8,256]{2,1,0:T(8,128)}), f32[32,8,256]{2,1,0:T(8,128)S(1)}, u32[]{:S(2)}, u32[]{:S(2)}) async-start(f32[32,8,256]{2,1,0:T(8,128)} %broadcast_in_dim.14), calls=%async_computation.1 | async-start | bytes 524288 | tf_op jit(solution)/shard_map/all_to_all | solution.py:231
  37.8 11.3 %copy-start.5 = (f32[1,8,16,256]{3,2,1,0:T(8,128)}, f32[1,8,16,256]{3,2,1,0:T(8,128)S(1)}, u32[]{:S(2)}) copy-start(f32[1,8,16,256]{3,2,1,0:T(8,128)S(1)} %collective-permute-done.2) | copy-start | bytes 393220
  37.8 11.3 %collective-permute-start.3 = (f32[2,8,16,256]{3,2,1,0:T(8,128)S(1)}, f32[2,8,16,256]{3,2,1,0:T(8,128)S(1)}, u32[]{:S(2)}, u32[]{:S(2)}) collective-permute-start(f32[2,8,16,256]{3,2,1,0:T(8,128)S(1)} %pad_maximum_fusion.2), channel_id=1, source_target_pairs={{0,128},{32,416},{64,192},{96,480},{128,256},{160,32},{192,320},{2... | collective-permute-start | bytes 786440 | tf_op jit(solution)/shard_map/ppermute | solution.py:251
  49.2 39.2 %collective-permute-start.4 = (f32[4,8,16,256]{3,2,1,0:T(8,128)S(1)}, f32[4,8,16,256]{3,2,1,0:T(8,128)}, u32[]{:S(2)}, u32[]{:S(2)}) collective-permute-start(f32[4,8,16,256]{3,2,1,0:T(8,128)S(1)} %pad_maximum_fusion.1), channel_id=1, source_target_pairs={{0,64},{32,480},{64,128},{96,32},{128,192},{160,96},{192,256},{224... | collective-permute-start | bytes 1572872 | tf_op jit(solution)/shard_map/ppermute | solution.py:251
  53.8 4.7 %copy-start.3 = (f32[32,8,256]{2,1,0:T(8,128)}, f32[32,8,256]{2,1,0:T(8,128)S(1)}, u32[]{:S(2)}) copy-start(f32[32,8,256]{2,1,0:T(8,128)S(1)} %all-to-all-done.1) | copy-start | bytes 786436
  56.6 28.5 %collective-permute-start = (f32[2,4,64,256]{3,2,1,0:T(8,128)}, f32[2,4,64,256]{3,2,1,0:T(8,128)S(1)}, u32[]{:S(2)}, u32[]{:S(2)}) collective-permute-start(f32[2,4,64,256]{3,2,1,0:T(8,128)} %dynamic-slice_bitcast_fusion), channel_id=1, source_target_pairs={{0,32},{32,0},{64,96},{96,64},{128,160},{160,128},{192,224},{224,1... | collective-permute-start | bytes 1572872 | tf_op jit(solution)/shard_map/ppermute | solution.py:270
  59.8 14.7 %all-to-all-start.2 = ((f32[16,8,256]{2,1,0:T(8,128)}), f32[16,8,256]{2,1,0:T(8,128)S(1)}, u32[]{:S(2)}, u32[]{:S(2)}) async-start(f32[16,8,256]{2,1,0:T(8,128)} %broadcast_in_dim.16), calls=%async_computation.2 | async-start | bytes 262144 | tf_op jit(solution)/shard_map/all_to_all | solution.py:231
  75.3 22.8 %all-to-all-start.3 = ((f32[32,8,256]{2,1,0:T(8,128)}), f32[32,8,256]{2,1,0:T(8,128)S(1)}, u32[]{:S(2)}, u32[]{:S(2)}) async-start(f32[32,8,256]{2,1,0:T(8,128)} %broadcast_in_dim.17), calls=%async_computation.3 | async-start | bytes 524288 | tf_op jit(solution)/shard_map/all_to_all | solution.py:231
  85.0 3.4 %copy-start.6 = (f32[1,8,16,256]{3,2,1,0:T(8,128)S(1)}, f32[1,8,16,256]{3,2,1,0:T(8,128)}, u32[]{:S(2)}) copy-start(f32[1,8,16,256]{3,2,1,0:T(8,128)} %copy-done.5) | copy-start | bytes 393220
  85.1 3.3 %copy-start.7 = (f32[2,4,64,256]{3,2,1,0:T(8,128)}, f32[2,4,64,256]{3,2,1,0:T(8,128)S(1)}, u32[]{:S(2)}) copy-start(f32[2,4,64,256]{3,2,1,0:T(8,128)S(1)} %collective-permute-done) | copy-start | bytes 1572868
  85.8 10.5 %collective-permute-start.1 = (f32[4,64,256]{2,1,0:T(8,128)}, f32[4,64,256]{2,1,0:T(8,128)}, u32[]{:S(2)}, u32[]{:S(2)}) collective-permute-start(f32[4,64,256]{2,1,0:T(8,128)} %bitcast_add_fusion), channel_id=1, source_target_pairs={{0,64},{32,96},{64,0},{96,32},{128,192},{160,224},{192,128},{224,1... | collective-permute-start | bytes 786440 | tf_op jit(solution)/shard_map/ppermute | solution.py:272
  89.5 21.2 %collective-permute-start.5 = (f32[8,8,16,256]{3,2,1,0:T(8,128)S(1)}, f32[8,8,16,256]{3,2,1,0:T(8,128)S(1)}, u32[]{:S(2)}, u32[]{:S(2)}) collective-permute-start(f32[8,8,16,256]{3,2,1,0:T(8,128)S(1)} %pad_maximum_fusion.s_ref), channel_id=1, source_target_pairs={{0,32},{32,0},{64,96},{96,64},{128,160},{160,128},{192,224},{224,1... | collective-permute-start | bytes 3145736 | tf_op jit(solution)/shard_map/ppermute | solution.py:252
  98.1 13.5 %all-to-all-start.4 = ((f32[4,64,256]{2,1,0:T(8,128)}), f32[4,64,256]{2,1,0:T(8,128)S(1)}, u32[]{:S(2)}, u32[]{:S(2)}) async-start(f32[4,64,256]{2,1,0:T(8,128)} %fusion.3), calls=%async_computation.4 | async-start | bytes 524288 | tf_op jit(solution)/shard_map/all_to_all | solution.py:231
  155.4 5.7 %copy-start.4 = (f32[32,8,256]{2,1,0:T(8,128)S(1)}, f32[32,8,256]{2,1,0:T(8,128)}, u32[]{:S(2)}) copy-start(f32[32,8,256]{2,1,0:T(8,128)} %copy-done.3) | copy-start | bytes 786436
  155.4 19.3 %all-to-all-start.7 = ((f32[32,8,384]{2,1,0:T(8,128)}), f32[32,8,384]{2,1,0:T(8,128)S(1)}, u32[]{:S(2)}, u32[]{:S(2)}) async-start(f32[32,8,384]{2,1,0:T(8,128)} %broadcast_in_dim.39), calls=%async_computation.7 | async-start | bytes 786432 | tf_op jit(solution)/shard_map/all_to_all | solution.py:231
